TPU v7x, 1024 devices: a whole 4x4x32 slice. The times are simulated.
1024 devices in a mesh: dp: 8 (over y, x_hi), vocab: 32 (over z), mp: 4 (over x_lo, core).
Axes of the slice: x: 4 (x_hi: 2, x_lo: 2; x = x_hi * 2 + x_lo), y: 4, z: 32, core: 2. Of those that a mesh axis runs over, the one named last changes fastest.
Arguments:
- hidden: bfloat16 [1024, 3584], P('dp', 'mp'), may hold values from -20 to 20
- head_weight: bfloat16 [3584, 152064], P('mp', ('dp', 'vocab')), may hold values from -1 to 1
- teacher_logits: bfloat16 [1024, 152064], P('mp', ('dp', 'vocab')), may hold values from -20 to 330
- response_start: int32 [4], replicated, may hold values from 0 to 128
Outputs:
- token_kl: float32 [1024], P('mp')
- grad_hidden: float32 [1024, 3584], P('dp', 'mp')
- grad_head: bfloat16 [3584, 152064], P('mp', ('dp', 'vocab'))
All inputs are finite; a program needn't handle non-finite values.
Results may differ from a plain program's by a relative error of at most 0.01.
Values may be sent and summed in bfloat16 or wider, within the bound.
A program may use at most 32 MiB of HBM per device.

v0:
```python
import jax
import jax.numpy as jnp
from jax import lax
from jax.sharding import PartitionSpec as P

LEN = 256


def per_device(hidden, head_weight, teacher_logits, response_start):
    gathered = lax.all_gather(hidden, "dp", axis=0, tiled=True)
    own_rows = gathered.shape[0] // lax.axis_size("mp")
    row_block = gathered
    student = lax.psum_scatter(
        jnp.dot(row_block, head_weight, preferred_element_type=jnp.float32),
        "mp",
        scatter_dimension=0,
        tiled=True,
    )
    target = teacher_logits.astype(jnp.float32)
    local_s = jnp.max(student, axis=1)
    local_t = jnp.max(target, axis=1)
    top_s, top_t = lax.pmax((local_s, local_t), ("dp", "vocab"))
    exp_s = jnp.exp(student - top_s[:, None])
    exp_t = jnp.exp(target - top_t[:, None])
    sum_s, sum_t, cross_term = lax.psum(
        (
            jnp.sum(exp_s, axis=1),
            jnp.sum(exp_t, axis=1),
            jnp.sum(exp_t * (target - student), axis=1),
        ),
        ("dp", "vocab"),
    )
    student_prob = exp_s / sum_s[:, None]
    teacher_prob = exp_t / sum_t[:, None]
    positions = lax.axis_index("mp") * own_rows + jnp.arange(own_rows, dtype=jnp.int32)
    sequence = positions // LEN
    seq_ids = jnp.arange(response_start.shape[0], dtype=jnp.int32)
    starts = jnp.sum(
        jnp.where(sequence[:, None] == seq_ids[None, :], response_start[None, :], 0), axis=1
    )
    response_mask = (positions % LEN >= starts).astype(jnp.float32)
    token_kl = response_mask * (
        cross_term / sum_t - top_t - jnp.log(sum_t) + top_s + jnp.log(sum_s)
    )
    logit_grads = (response_mask[:, None] * (student_prob - teacher_prob)).astype(jnp.bfloat16)
    all_grads = lax.all_gather(logit_grads, "mp", axis=0, tiled=True)
    grad_head = lax.dot_general(
        gathered, all_grads, (((0,), (0,)), ((), ())), preferred_element_type=jnp.float32
    ).astype(jnp.bfloat16)
    row_block = all_grads
    dp_share = lax.psum_scatter(
        lax.dot_general(
            row_block, head_weight, (((1,), (1,)), ((), ())), preferred_element_type=jnp.float32
        ),
        "dp",
        scatter_dimension=0,
        tiled=True,
    )
    grad_hidden = lax.psum(dp_share, "vocab")
    return (token_kl, grad_hidden, grad_head)


def solution(mesh):
    return jax.shard_map(
        per_device,
        mesh=mesh,
        in_specs=(P("dp", "mp"), P("mp", ("dp", "vocab")), P("mp", ("dp", "vocab")), P()),
        out_specs=(P("mp"), P("dp", "mp"), P("mp", ("dp", "vocab"))),
        check_vma=False,
    )
```

profile of v0, /device:TPU:6, one launch (start us, length us, event | category | flops | bytes accessed | tf_op | source)
XLA Modules:
  0.0 1991.9 jit_solution(13164395727258132736)
XLA Ops:
  7.2 0.0 all-gather.3.cloned.1.call-start
  7.2 0.7 all-gather.3.cloned.1.call-update
  7.9 0.0 reduce-scatter.3.cloned.1.call-start
  8.0 97.9 %all-gather.3.cloned.1.call-done = bf16[1024,896]{1,0:T(8,128)(2,1)} async-done(((bf16[128,896]{1,0:T(8,128)(2,1)}), bf16[1024,896]{1,0:T(8,128)(2,1)}) %all-gather.3.cloned.1.call-update) | async-done | bytes 1835024 | tf_op jit(solution)/shard_map/all_gather | solution.py:10
  105.9 4.4 fusion.14
  110.3 0.0 all-gather.5.cloned.1.call-start
  110.4 0.9 copy-done.2
  111.2 0.1 reduce_max.23
  111.4 0.1 select_reduce_fusion
  111.5 47.4 %reduce-scatter.3.cloned.1.call-done = f32[256,594]{0,1:T(8,128)} async-done(((f32[1024,594]{0,1:T(8,128)}), f32[256,594]{0,1:T(8,128)}) %reduce-scatter.3.cloned.1.call-update) | async-done | bytes 608272 | tf_op jit(solution)/shard_map/reduce_scatter | solution.py:13
  158.8 1.2 reduce_max.25
  160.1 625.1 %all-reduce.1 = (f32[256]{0:T(256)S(1)}, f32[256]{0:T(256)S(1)}) all-reduce(bf16[256]{0:T(256)(128)(2,1)S(1)} %reduce_max.23, f32[256]{0:T(256)S(1)} %reduce_max.25), channel_id=1, replica_groups=mesh['dp'=8,'vocab'=32,'mp'=4] {'dp','vocab'}, use_global_device_ids=true, to_apply=%region_2.0 | all-reduce | flops 512 | bytes 3584 | tf_op jit(solution)/shard_map/pmax | solution.py:22
  785.1 1.3 fusion.5
  786.5 701.9 %all-reduce = (f32[256]{0:T(256)S(1)}, f32[256]{0:T(256)S(1)}, f32[256]{0:T(256)S(1)}) all-reduce(f32[256]{0:T(256)S(1)} %get-tuple-element.4, f32[256]{0:T(256)S(1)} %get-tuple-element.5, f32[256]{0:T(256)S(1)} %get-tuple-element.3), channel_id=1, replica_groups=mesh['dp'=8,'vocab'=32,'mp'=4] {'dp','vocab'}, use_global_device_ids=true, to_apply=%region_11.12 | all-reduce | flops 768 | bytes 6144 | tf_op jit(solution)/shard_map/psum | solution.py:25
  1488.4 1.0 fusion.8
  1489.3 0.0 reduce-scatter.5.cloned.1.call-start
  1489.4 104.3 %all-gather.5.cloned.1.call-done = bf16[1024,594]{0,1:T(8,128)(2,1)} async-done(((bf16[256,594]{0,1:T(8,128)(2,1)}), bf16[1024,594]{0,1:T(8,128)(2,1)}) %all-gather.5.cloned.1.call-update) | async-done | bytes 1216528 | tf_op jit(solution)/shard_map/all_gather | solution.py:46
  1593.7 4.9 fusion.15
  1598.6 0.0 all-reduce.4.cloned.1.call-start
  1598.6 118.7 %reduce-scatter.5.cloned.1.call-done = f32[128,896]{1,0:T(8,128)} async-done(((f32[1024,896]{1,0:T(8,128)}), f32[128,896]{1,0:T(8,128)}) %reduce-scatter.5.cloned.1.call-update) | async-done | bytes 458768 | tf_op jit(solution)/shard_map/reduce_scatter | solution.py:51
  1717.3 0.6 add_select_fusion
  1717.9 3.7 fusion
  1721.6 261.9 %all-reduce.4.cloned.1.call-done = f32[128,896]{1,0:T(8,128)} async-done(((f32[128,896]{1,0:T(8,128)}), f32[128,896]{1,0:T(8,128)}) %all-reduce.4.cloned.1.call-update) | async-done | bytes 458768 | tf_op jit(solution)/shard_map/psum | solution.py:59
  1983.5 1.8 copy.8
  (15 shorter events, 0.1 us)
Async XLA Ops:
  7.2 98.7 %copy-start = (bf16[896,594]{0,1:T(8,128)(2,1)S(1)}, bf16[896,594]{0,1:T(8,128)(2,1)}, u32[]{:S(2)}) copy-start(bf16[896,594]{0,1:T(8,128)(2,1)} %param.5) | copy-start | bytes 3193348
  7.2 98.7 %all-gather.3.cloned.1.call-start = ((), (), s32[]{:S(2)}) async-start(), calls=%async_computation.2 | async-start | bytes 2064384 | tf_op jit(solution)/shard_map/all_gather | solution.py:10
  7.9 150.9 %reduce-scatter.3.cloned.1.call-start = ((), (), s32[]{:S(2)}) async-start(), calls=%async_computation.3 | async-start | bytes 3072000 | tf_op jit(solution)/shard_map/reduce_scatter | solution.py:13
  110.3 1.0 copy-start.2
  110.3 1.1 copy-start.3
  110.3 1483.3 %all-gather.5.cloned.1.call-start = ((), (), s32[]{:S(2)}) async-start(), calls=%async_computation.4 | async-start | bytes 1536000 | tf_op jit(solution)/shard_map/all_gather | solution.py:46
  158.8 1329.5 %copy-start.1 = (f32[256,594]{0,1:T(8,128)S(1)}, f32[256,594]{0,1:T(8,128)}, u32[]{:S(2)}) copy-start(f32[256,594]{0,1:T(8,128)} %reduce-scatter.3.cloned.1.call-done) | copy-start | bytes 1824772
  1489.3 227.9 %reduce-scatter.5.cloned.1.call-start = ((), (), s32[]{:S(2)}) async-start(), calls=%async_computation.5 | async-start | bytes 4128768 | tf_op jit(solution)/shard_map/reduce_scatter | solution.py:51
  1598.5 119.3 %copy-start.4 = (bf16[1024,896]{1,0:T(8,128)(2,1)S(1)}, bf16[1024,896]{1,0:T(8,128)(2,1)}, u32[]{:S(2)}) copy-start(bf16[1024,896]{1,0:T(8,128)(2,1)} %all-gather.3.cloned.1.call-done) | copy-start | bytes 5505028
  1598.6 385.0 %all-reduce.4.cloned.1.call-start = ((), (), s32[]{:S(2)}) async-start(), calls=%async_computation.6 | async-start | bytes 917504 | tf_op jit(solution)/shard_map/psum | solution.py:59
Sparse Core Ops, SparseCore 0:
  12.3 93.4 all-gather.2
  110.4 48.3 reduce-scatter.2
  1489.5 104.1 all-gather.4
  1599.4 117.7 reduce-scatter.4
  1719.4 264.0 all-reduce.3
where the time goes:
time: 1990 us
  blocking collectives  1330 us (67%)
  waiting for transfers between devices  631 us (32%)
    psum x1, blocking collectives, per_device(): lax.psum((jnp.sum(exp_s, axis=1), jnp.sum(exp_t, axis=1), jnp.sum(exp_t *...  702 us
    pmax x1, blocking collectives, per_device(): top_s, top_t = lax.pmax((local_s, local_t), ('dp', 'vocab'))  625 us
    psum x1, waiting for transfers between devices, per_device(): grad_hidden = lax.psum(dp_share, 'vocab')  262 us
    reduce_scatter x1, waiting for transfers between devices, per_device(): lax.psum_scatter(lax.dot_general(row_block, head_weight, (((1,), (1,)), (...  119 us
    all_gather x1, waiting for transfers between devices, per_device(): all_grads = lax.all_gather(logit_grads, 'mp', axis=0, tiled=True)  104 us
    all_gather x1, waiting for transfers between devices, per_device(): gathered = lax.all_gather(hidden, 'dp', axis=0, tiled=True)  97.9 us
    reduce_scatter x1, waiting for transfers between devices, per_device(): lax.psum_scatter(jnp.dot(row_block, head_weight, preferred_element_type=j...  47.4 us
  transfers between devices with their start and end apart: 5, of which 5 were waited for; matrix products, arithmetic and copies ran while one was open for 0% of the time, Pallas kernels for 0%

commit v1 on v0

v1 whole, which is shorter than its diff:
```python
import functools

import jax
import jax.numpy as jnp
from jax import lax
from jax.experimental import pallas as pl
from jax.experimental.pallas import tpu as pltpu
from jax.sharding import PartitionSpec as P

LEN = 256
MESH = pl.DeviceIdType.MESH
F32 = jnp.float32
BF16 = jnp.bfloat16

ROW_MS, ROW_SS, ROW_MT, ROW_ST, ROW_C = range(5)


class Group:
    def __init__(self, n, me, device):
        self.n, self.me, self.device = n, me, device

    def others(self):
        return [lax.rem(self.me + k, self.n) for k in range(1, self.n)]

    def copy(self, src, dst, send, recv, to):
        return pltpu.make_async_remote_copy(
            src_ref=src,
            dst_ref=dst,
            send_sem=send,
            recv_sem=recv,
            device_id=self.device(to),
            device_id_type=MESH,
        )


def gather_start(group, src, held, send, recv):
    for peer in group.others():
        group.copy(src, held.at[group.me], send.at[peer], recv.at[group.me], peer).start()


def gather_wait(group, src, held, send, recv):
    for peer in group.others():
        copy = group.copy(src, held.at[peer], send.at[peer], recv.at[peer], peer)
        copy.wait_recv()
        copy.wait_send()


def scatter_start(group, parts, held, send, recv):
    for peer in group.others():
        group.copy(parts.at[peer], held.at[group.me], send.at[peer], recv.at[group.me], peer).start()


def scatter_wait(group, parts, held, send, recv):
    for peer in group.others():
        copy = group.copy(parts.at[peer], held.at[peer], send.at[peer], recv.at[peer], peer)
        copy.wait_recv()
        copy.wait_send()


def merge(held, n):
    rows = [[held[i, r : r + 1, :] for r in range(5)] for i in range(n)]
    top_s = functools.reduce(jnp.maximum, [row[ROW_MS] for row in rows])
    top_t = functools.reduce(jnp.maximum, [row[ROW_MT] for row in rows])
    sum_s = sum_t = cross = None
    for row in rows:
        scale_s = jnp.exp(row[ROW_MS] - top_s)
        scale_t = jnp.exp(row[ROW_MT] - top_t)
        terms = row[ROW_SS] * scale_s, row[ROW_ST] * scale_t, row[ROW_C] * scale_t
        if sum_s is None:
            sum_s, sum_t, cross = terms
        else:
            sum_s, sum_t, cross = sum_s + terms[0], sum_t + terms[1], cross + terms[2]
    return top_s, sum_s, top_t, sum_t, cross


def store_stats(ref, stats):
    for row, value in enumerate(stats):
        ref[row : row + 1, :] = value


def kernel(
    sizes,
    hidden_ref, head_ref, teacher_ref, start_ref,
    kl_ref, grad_hidden_ref, grad_head_ref,
    hid, keep, swap_out, swap_in, cross_out, cross_in, stud,
    st_dp, st_zl, st_zh, grads, gh_out, gh_in, acc,
    zl_out, zl_in, zh_out, zh_in, fin_h, fin_l, head_acc,
    local_sem, hid_s, hid_r, swap_s, swap_r, cross_s, cross_r,
    sdp_s, sdp_r, szl_s, szl_r, szh_s, szh_r,
    gx_s, gx_r, gc_s, gc_r, gd_s, gd_r, gh_s, gh_r,
    zl_s, zl_r, zh_s, zh_r, fh_s, fh_r, fl_s, fl_r,
):
    n_dp, n_zl, n_zh = sizes
    tok = hidden_ref.shape[0]
    d, z, m = lax.axis_index("dp"), lax.axis_index("vocab"), lax.axis_index("mp")
    x, c = m // 2, m % 2
    zl, zh = z % n_zl, z // n_zl
    other_core, other_chip = 2 * x + (1 - c), 2 * (1 - x) + c
    diagonal = 2 * (1 - x) + (1 - c)

    dp = Group(n_dp, d, lambda i: (i, z, m))
    near = Group(n_zl, zl, lambda i: (d, zh * n_zl + i, m))
    far = Group(n_zh, zh, lambda i: (d, i * n_zl + zl, m))
    mp = Group(4, m, lambda i: (d, z, i))

    barrier = pltpu.get_barrier_semaphore()
    peers = [g.device(p) for g in (dp, near, far) for p in g.others()]
    peers += [mp.device(other_core), mp.device(other_chip)]
    for peer in peers:
        pl.semaphore_signal(barrier, inc=1, device_id=peer, device_id_type=MESH)
    own = pltpu.make_async_copy(hidden_ref, hid.at[d], local_sem)
    own.start()
    pl.semaphore_wait(barrier, len(peers))

    gather_start(dp, hidden_ref, hid, hid_s, hid_r)

    own.wait()
    gather_wait(dp, hidden_ref, hid, hid_s, hid_r)

    def swap(k):
        return mp.copy(swap_out.at[k], swap_in.at[k], swap_s.at[k], swap_r.at[k], other_core)

    def cross(k):
        return mp.copy(cross_out.at[k], cross_in.at[k], cross_s.at[k], cross_r.at[k], other_chip)

    def partial(block):
        return lax.dot_general(
            head_ref[...], hid[block], (((1,), (1,)), ((), ())), preferred_element_type=F32
        )

    def student_step(k, carry):
        half = k % 2
        chip = jnp.where(k < 2, 1 - x, x)
        swap_out[k] = partial(2 * (2 * chip + 1 - c) + half)
        swap(k).start()
        keep[k] = partial(2 * (2 * chip + c) + half)
        return carry

    lax.fori_loop(0, 4, student_step, 0)
    for k in range(2):
        swap(k).wait()
        cross_out[k] = keep[k] + swap_in[k]
        cross(k).start()
    for k in range(2):
        swap(2 + k).wait()
        keep[2 + k] = keep[2 + k] + swap_in[2 + k]

    for h in range(2):
        cols = slice(h * tok, (h + 1) * tok)
        cross(h).wait()
        s = keep[2 + h] + cross_in[h]
        stud[h] = s
        t = teacher_ref[:, cols].astype(F32)
        top_s = jnp.max(s, axis=0, keepdims=True)
        top_t = jnp.max(t, axis=0, keepdims=True)
        exp_t = jnp.exp(t - top_t)
        stats = (
            top_s,
            jnp.sum(jnp.exp(s - top_s), axis=0, keepdims=True),
            top_t,
            jnp.sum(exp_t, axis=0, keepdims=True),
            jnp.sum(exp_t * (t - s), axis=0, keepdims=True),
        )
        for row, value in enumerate(stats):
            st_dp[d, row : row + 1, cols] = value
    for group, held, send, recv, to in (
        (dp, st_dp, sdp_s, sdp_r, st_zl.at[zl]),
        (near, st_zl, szl_s, szl_r, st_zh.at[zh]),
        (far, st_zh, szh_s, szh_r, None),
    ):
        gather_start(group, held.at[group.me], held, send, recv)
        gather_wait(group, held.at[group.me], held, send, recv)
        stats = merge(held, group.n)
        if to is not None:
            store_stats(to, stats)
    top_s, sum_s, top_t, sum_t, cross_term = stats
    position = lax.broadcasted_iota(jnp.int32, (1, 2 * tok), 1)
    mask = jnp.where(position >= start_ref[m], 1.0, 0.0).astype(F32)
    kl_ref[...] = mask * (cross_term / sum_t - top_t - jnp.log(sum_t) + top_s + jnp.log(sum_s))
    scale_s, scale_t = mask / sum_s, mask / sum_t

    def grad_x(h):
        block = grads.at[2 * m + h]
        return mp.copy(block, block, gx_s.at[h], gx_r.at[h], other_chip)

    def grad_c(h):
        block = grads.at[2 * m + h]
        return mp.copy(block, block, gc_s.at[h], gc_r.at[h], other_core)

    def grad_d(h):
        block = grads.at[2 * other_chip + h]
        return mp.copy(block, block, gd_s.at[h], gd_r.at[h], other_core)

    for h in range(2):
        cols = slice(h * tok, (h + 1) * tok)
        exp_s = jnp.exp(stud[h] - top_s[:, cols])
        exp_t = jnp.exp(teacher_ref[:, cols].astype(F32) - top_t[:, cols])
        grads[2 * m + h] = (exp_s * scale_s[:, cols] - exp_t * scale_t[:, cols]).astype(BF16)
        grad_x(h).start()
        grad_c(h).start()

    def owner_copy(block):
        return dp.copy(gh_out.at[block], gh_in.at[d], gh_s.at[block], gh_r.at[d], block)

    def hidden_terms(block):
        gh_out[block] = lax.dot_general(
            grads[block], head_ref[...], (((0,), (0,)), ((), ())), preferred_element_type=F32
        ).astype(BF16)

        @pl.when(block != d)
        def _():
            owner_copy(block).start()

    for h in range(2):
        hidden_terms(2 * m + h)
    for h in range(2):
        grad_c(h).wait()
        hidden_terms(2 * other_core + h)
    for h in range(2):
        grad_x(h).wait()
        grad_d(h).start()
        hidden_terms(2 * other_chip + h)
    for h in range(2):
        grad_d(h).wait()
        hidden_terms(2 * diagonal + h)

    head_acc[...] = jnp.zeros_like(head_acc)

    def head_step(block, carry):
        head_acc[...] += jnp.dot(grads[block], hid[block], preferred_element_type=F32)
        return carry

    lax.fori_loop(0, n_dp, head_step, 0)
    grad_head_ref[...] = head_acc[...].astype(BF16)

    scatter_wait(dp, gh_out, gh_in, gh_s, gh_r)
    gh_in[d] = gh_out[d]
    total = gh_in[0].astype(F32)
    for i in range(1, n_dp):
        total = total + gh_in[i].astype(F32)

    rows = tok // n_zl
    for i in range(n_zl):
        acc[i] = total[i * rows : (i + 1) * rows, :]
        zl_out[i] = acc[i].astype(BF16)
    scatter_start(near, zl_out, zl_in, zl_s, zl_r)
    scatter_wait(near, zl_out, zl_in, zl_s, zl_r)
    total = acc[zl]
    for peer in near.others():
        total = total + zl_in[peer].astype(F32)
    few = rows // n_zh
    for i in range(n_zh):
        zh_out[i] = total[i * few : (i + 1) * few, :]
    scatter_start(far, zh_out, zh_in, zh_s, zh_r)
    scatter_wait(far, zh_out, zh_in, zh_s, zh_r)
    zh_in[zh] = zh_out[zh]
    total = zh_in[0]
    for i in range(1, n_zh):
        total = total + zh_in[i]
    fin_h[zh] = total
    gather_start(far, fin_h.at[zh], fin_h, fh_s, fh_r)
    gather_wait(far, fin_h.at[zh], fin_h, fh_s, fh_r)
    for i in range(n_zh):
        fin_l[zl, i * few : (i + 1) * few, :] = fin_h[i]
    gather_start(near, fin_l.at[zl], fin_l, fl_s, fl_r)
    gather_wait(near, fin_l.at[zl], fin_l, fl_s, fl_r)
    for i in range(n_zl):
        grad_hidden_ref[i * rows : (i + 1) * rows, :] = fin_l[i]


def solution(mesh):
    n_dp, n_z, n_mp = mesh.shape["dp"], mesh.shape["vocab"], mesh.shape["mp"]
    n_zl = min(4, n_z)
    n_zh = n_z // n_zl

    def per_device(hidden, head_weight, teacher_logits, response_start):
        tok, depth = hidden.shape
        own, cols = teacher_logits.shape
        assert n_mp == 4 and own == 2 * tok == LEN and n_dp == 8
        rows = tok // n_zl
        few = rows // n_zh
        dma = pltpu.SemaphoreType.DMA
        vmem = pl.BlockSpec(memory_space=pltpu.VMEM)
        kl, grad_hidden, grad_head = pl.pallas_call(
            functools.partial(kernel, (n_dp, n_zl, n_zh)),
            name="distill",
            out_shape=(
                jax.ShapeDtypeStruct((1, own), F32),
                jax.ShapeDtypeStruct((tok, depth), F32),
                jax.ShapeDtypeStruct((cols, depth), BF16),
            ),
            in_specs=[vmem, vmem, vmem, pl.BlockSpec(memory_space=pltpu.SMEM)],
            out_specs=(vmem, vmem, vmem),
            scratch_shapes=[
                pltpu.VMEM((n_dp, tok, depth), BF16),
                pltpu.VMEM((4, cols, tok), F32),
                pltpu.VMEM((4, cols, tok), F32),
                pltpu.VMEM((4, cols, tok), F32),
                pltpu.VMEM((2, cols, tok), F32),
                pltpu.VMEM((2, cols, tok), F32),
                pltpu.VMEM((2, cols, tok), F32),
                pltpu.VMEM((n_dp, 8, own), F32),
                pltpu.VMEM((n_zl, 8, own), F32),
                pltpu.VMEM((n_zh, 8, own), F32),
                pltpu.VMEM((n_dp, cols, tok), BF16),
                pltpu.VMEM((n_dp, tok, depth), BF16),
                pltpu.VMEM((n_dp, tok, depth), BF16),
                pltpu.VMEM((n_zl, rows, depth), F32),
                pltpu.VMEM((n_zl, rows, depth), BF16),
                pltpu.VMEM((n_zl, rows, depth), BF16),
                pltpu.VMEM((n_zh, few, depth), F32),
                pltpu.VMEM((n_zh, few, depth), F32),
                pltpu.VMEM((n_zh, few, depth), F32),
                pltpu.VMEM((n_zl, rows, depth), F32),
                pltpu.VMEM((cols, depth), F32),
                dma,
                dma((n_dp,)), dma((n_dp,)),
                dma((4,)), dma((4,)),
                dma((2,)), dma((2,)),
                dma((n_dp,)), dma((n_dp,)),
                dma((n_zl,)), dma((n_zl,)),
                dma((n_zh,)), dma((n_zh,)),
                dma((2,)), dma((2,)),
                dma((2,)), dma((2,)),
                dma((2,)), dma((2,)),
                dma((n_dp,)), dma((n_dp,)),
                dma((n_zl,)), dma((n_zl,)),
                dma((n_zh,)), dma((n_zh,)),
                dma((n_zh,)), dma((n_zh,)),
                dma((n_zl,)), dma((n_zl,)),
            ],
            compiler_params=pltpu.CompilerParams(
                collective_id=0, has_side_effects=True, vmem_limit_bytes=56 << 20
            ),
        )(hidden, head_weight.T, teacher_logits.T, response_start)
        return kl.reshape(own), grad_hidden, grad_head.T

    return jax.shard_map(
        per_device,
        mesh=mesh,
        in_specs=(P("dp", "mp"), P("mp", ("dp", "vocab")), P("mp", ("dp", "vocab")), P()),
        out_specs=(P("mp"), P("dp", "mp"), P("mp", ("dp", "vocab"))),
        check_vma=False,
    )
```

time: 1990 us -> 178 us (0.09)
  blocking collectives: 1330 us -> 0 us
  waiting for transfers between devices: 631 us -> 0 us
  Pallas kernels: 0 us -> 172 us
    psum x1 -> x0, blocking collectives: 702 us -> none  [per_device(): lax.psum((jnp.sum(exp_s, axis=1), jnp.sum(exp_t, axis=1), jnp.sum(exp_t *...]
    pmax x1 -> x0, blocking collectives: 625 us -> none  [per_device(): top_s, top_t = lax.pmax((local_s, local_t), ('dp', 'vocab'))]
    psum x1 -> x0, waiting for transfers between devices: 262 us -> none  [per_device(): grad_hidden = lax.psum(dp_share, 'vocab')]
    all_gather x2 -> x0, waiting for transfers between devices: 202 us -> none  [the longest x1 104 us: per_device(): all_grads = lax.all_gather(logit_grads, 'mp', axis=0, tiled=True)]
    pallas_call x0 -> x1, Pallas kernels: none -> 172 us  [per_device(): pl.pallas_call(functools.partial(kernel, (n_dp, n_zl, n_zh)), name='disti...]
    reduce_scatter x2 -> x0, waiting for transfers between devices: 166 us -> none  [the longest x1 119 us: per_device(): lax.psum_scatter(lax.dot_general(row_block, head_weight, (((1,), (1,)), (...]
  transfers between devices with their start and end apart: 5 -> 0, of which waited for: 5 -> 0; matrix products, arithmetic and copies ran while one was open for 0% -> 0% of each run, Pallas kernels for 0% -> 0%
where the time goes in v1:
time: 178 us
  Pallas kernels  172 us (97%)
  local copies, waits for them, and re-layouts  5.34 us (3%)
    pallas_call x1, Pallas kernels, per_device(): pl.pallas_call(functools.partial(kernel, (n_dp, n_zl, n_zh)), name='disti...  172 us
    unnamed x3, local copies, waits for them, and re-layouts  5.34 us

profile of v1, /device:TPU:6, one launch (start us, length us, event | category | flops | bytes accessed | tf_op | source)
XLA Modules:
  0.0 177.7 jit_solution(71076156090657893)
XLA Ops:
  0.6 171.7 %distill.1 = (f32[1,256]{1,0:T(1,128)}, f32[128,896]{1,0:T(8,128)}, bf16[594,896]{1,0:T(8,128)(2,1)}) custom-call(bf16[128,896]{1,0:T(8,128)(2,1)} %hidden_ref.1, bf16[594,896]{1,0:T(8,128)(2,1)} %bitcast.4, bf16[594,256]{1,0:T(8,128)(2,1)} %bitcast.6, s32[4]{0:T(128)} %start_ref.1), custom_call_target="tpu_custom_call" | custom-call | tf_op jit(solution)/shard_map/distill/pallas_call | solution.py:284
  172.4 1.2 copy.10
  173.6 1.8 %copy.11 = f32[128,896]{1,0:T(8,128)} copy(f32[128,896]{1,0:T(8,128)} %get-tuple-element.13) | data formatting | bytes 917504
  175.4 2.3 %copy.12 = bf16[896,594]{0,1:T(8,128)(2,1)} copy(bf16[896,594]{0,1:T(8,128)(2,1)} %bitcast.5) | data formatting | bytes 2128896

commit v2 on v1

v2 whole, which is shorter than its diff:
```python
import functools

import jax
import jax.numpy as jnp
from jax import lax
from jax.experimental import pallas as pl
from jax.experimental.pallas import tpu as pltpu
from jax.sharding import PartitionSpec as P

LEN = 256
MESH = pl.DeviceIdType.MESH
F32 = jnp.float32
BF16 = jnp.bfloat16

ROW_MS, ROW_SS, ROW_MT, ROW_ST, ROW_C = range(5)


class Group:
    def __init__(self, n, me, device):
        self.n, self.me, self.device = n, me, device

    def others(self):
        return [lax.rem(self.me + k, self.n) for k in range(1, self.n)]

    def copy(self, src, dst, send, recv, to):
        return pltpu.make_async_remote_copy(
            src_ref=src,
            dst_ref=dst,
            send_sem=send,
            recv_sem=recv,
            device_id=self.device(to),
            device_id_type=MESH,
        )


def gather_start(group, src, held, send, recv):
    for peer in group.others():
        group.copy(src, held.at[group.me], send.at[peer], recv.at[group.me], peer).start()


def gather_wait(group, src, held, send, recv):
    for peer in group.others():
        copy = group.copy(src, held.at[peer], send.at[peer], recv.at[peer], peer)
        copy.wait_recv()
        copy.wait_send()


def scatter_start(group, parts, held, send, recv):
    for peer in group.others():
        group.copy(parts.at[peer], held.at[group.me], send.at[peer], recv.at[group.me], peer).start()


def scatter_wait(group, parts, held, send, recv):
    for peer in group.others():
        copy = group.copy(parts.at[peer], held.at[peer], send.at[peer], recv.at[peer], peer)
        copy.wait_recv()
        copy.wait_send()


def merge(held, n):
    rows = [[held[i, r : r + 1, :] for r in range(5)] for i in range(n)]
    top_s = functools.reduce(jnp.maximum, [row[ROW_MS] for row in rows])
    top_t = functools.reduce(jnp.maximum, [row[ROW_MT] for row in rows])
    sum_s = sum_t = cross = None
    for row in rows:
        scale_s = jnp.exp(row[ROW_MS] - top_s)
        scale_t = jnp.exp(row[ROW_MT] - top_t)
        terms = row[ROW_SS] * scale_s, row[ROW_ST] * scale_t, row[ROW_C] * scale_t
        if sum_s is None:
            sum_s, sum_t, cross = terms
        else:
            sum_s, sum_t, cross = sum_s + terms[0], sum_t + terms[1], cross + terms[2]
    return top_s, sum_s, top_t, sum_t, cross


def store_stats(ref, stats):
    for row, value in enumerate(stats):
        ref[row : row + 1, :] = value


def kernel(
    sizes,
    hidden_ref, head_hbm, teacher_hbm, start_ref,
    kl_ref, grad_hidden_ref, grad_head_hbm,
    head_ref, teacher_ref, head_out,
    hid, parts, swap_in, cross_out, cross_in, stud,
    st_dp, st_zl, st_zh, grads, gh_out, gh_in, acc,
    zl_out, zl_in, zh_out, zh_in, fin_h, fin_f, fin_l, head_acc,
    local_sem, ready, hx_s, hx_r, hy_s, hy_r, hz_s, hz_r,
    swap_s, swap_r, cross_s, cross_r,
    sdp_s, sdp_r, szl_s, szl_r, szh_s, szh_r,
    gx_s, gx_r, gc_s, gc_r, gd_s, gd_r, gh_s, gh_r,
    zl_s, zl_r, zh_s, zh_r, fh_s, fh_r, fl_s, fl_r,
):
    n_dp, n_z, n_zl, n_zh = sizes
    n_y = n_dp // 2
    sub, depth = hidden_ref.shape[1:]
    tok = 4 * sub
    d, z, m = lax.axis_index("dp"), lax.axis_index("vocab"), lax.axis_index("mp")
    x, c = m // 2, m % 2
    y = d // 2
    partner = 2 * y + (1 - d % 2)
    zl, zh = z % n_zl, z // n_zl
    other_core, other_chip = 2 * x + (1 - c), 2 * (1 - x) + c
    diagonal = 2 * (1 - x) + (1 - c)
    up, down = lax.rem(z + 1, n_z), lax.rem(z + n_z - 1, n_z)

    dp = Group(n_dp, d, lambda i: (i, z, m))
    column = Group(n_y, y, lambda i: (2 * i + d % 2, z, m))
    ring = Group(n_z, z, lambda i: (d, i, m))
    near = Group(n_zl, zl, lambda i: (d, zh * n_zl + i, m))
    far = Group(n_zh, zh, lambda i: (d, i * n_zl + zl, m))
    mp = Group(4, m, lambda i: (d, z, i))
    far_next = [far.device(lax.rem(zh + k, n_zh)) for k in (1, n_zh - 1)]

    barrier = pltpu.get_barrier_semaphore()
    peers = [g.device(p) for g in (dp, near) for p in g.others()] + far_next
    peers += [mp.device(other_core), mp.device(other_chip), ring.device(up), ring.device(down)]
    for peer in peers:
        pl.semaphore_signal(barrier, inc=1, device_id=peer, device_id_type=MESH)
    own = pltpu.make_async_copy(hidden_ref, hid.at[d], local_sem.at[0])
    own.start()
    load_head = pltpu.make_async_copy(head_hbm, head_ref, local_sem.at[1])
    load_head.start()
    load_teacher = pltpu.make_async_copy(teacher_hbm, teacher_ref, local_sem.at[2])
    load_teacher.start()
    own.wait()
    pl.semaphore_wait(barrier, len(peers))

    def tell(r):
        for peer in far_next:
            pl.semaphore_signal(ready.at[r], inc=1, device_id=peer, device_id_type=MESH)

    def hear(r):
        pl.semaphore_wait(ready.at[r], 2)

    half = pl.ds(2 * (z % 2), 2)

    def to_partner(block):
        part = hid.at[block, half]
        return dp.copy(part, part, hx_s, hx_r, partner)

    def to_column(block, peer):
        part = hid.at[block, half]
        return column.copy(part, part, hy_s.at[block % 2, peer], hy_r.at[block], peer)

    def to_ring(block, side, parity):
        part = hid.at[block, 2 * parity + side]
        return ring.copy(part, part, hz_s.at[block, side], hz_r.at[block, side], (up, down)[side])

    def pass_on(block):
        for side in range(2):
            to_ring(block, side, z % 2).start()

    to_partner(d).start()
    for i in range(2):
        block = 2 * y + i

        @pl.when(block != d)
        def _():
            to_partner(partner).wait_recv()

        for peer in column.others():
            to_column(block, peer).start()
    pass_on(partner)
    if n_zh >= 4:
        tell(0)

    def blocks_of(i):
        return [2 * row + i for row in column.others()]

    def forward(i):
        for block in blocks_of(i):
            to_column(block, block // 2).wait_recv()
            pass_on(block)

    def arrive(i):
        for block in blocks_of(i):
            for side in range(2):
                to_ring(block, side, 1 - z % 2).wait_recv()

        @pl.when(2 * y + i != d)
        def _():
            for side in range(2):
                to_ring(partner, side, 1 - z % 2).wait_recv()

    def swap(k):
        return mp.copy(parts.at[k, 0], swap_in.at[k], swap_s.at[k], swap_r.at[k], other_core)

    def cross(k):
        return mp.copy(cross_out.at[k], cross_in.at[k], cross_s.at[k], cross_r.at[k], other_chip)

    def partial_sums(k):
        chip = (1 - x) if k < 2 else x

        def one(j, carry):
            core = jnp.where(j == 0, 1 - c, c)
            block = hid[2 * (2 * chip + core) + k % 2].reshape(tok, depth)
            parts[k, j] = lax.dot_general(
                head_ref[...], block, (((1,), (1,)), ((), ())), preferred_element_type=F32
            )
            return carry

        lax.fori_loop(0, 2, one, 0)
        swap(k).start()

    def send_cross(k):
        swap(k).wait()
        cross_out[k] = parts[k, 1] + swap_in[k]
        cross(k).start()

    forward(0)
    load_head.wait()
    arrive(0)
    partial_sums(0)
    send_cross(0)
    if n_zh >= 4:
        hear(0)
        tell(1)
    forward(1)
    arrive(1)
    partial_sums(1)
    send_cross(1)
    if n_zh >= 4:
        hear(1)
        tell(2)
    partial_sums(2)
    partial_sums(3)
    load_teacher.wait()

    for h in range(2):
        cols = slice(h * tok, (h + 1) * tok)
        swap(2 + h).wait()
        stud[h] = parts[2 + h, 1] + swap_in[2 + h]
        cross(h).wait()
        s = stud[h] + cross_in[h]
        stud[h] = s
        t = teacher_ref[:, cols].astype(F32)
        top_s = jnp.max(s, axis=0, keepdims=True)
        top_t = jnp.max(t, axis=0, keepdims=True)
        exp_t = jnp.exp(t - top_t)
        stats = (
            top_s,
            jnp.sum(jnp.exp(s - top_s), axis=0, keepdims=True),
            top_t,
            jnp.sum(exp_t, axis=0, keepdims=True),
            jnp.sum(exp_t * (t - s), axis=0, keepdims=True),
        )
        for row, value in enumerate(stats):
            st_dp[d, row : row + 1, cols] = value

    def share(group, held, send, recv):
        gather_start(group, held.at[group.me], held, send, recv)
        gather_wait(group, held.at[group.me], held, send, recv)
        return merge(held, group.n)

    store_stats(st_zl.at[zl], share(dp, st_dp, sdp_s, sdp_r))
    store_stats(st_zh.at[zh], share(near, st_zl, szl_s, szl_r))
    if n_zh >= 4:
        hear(2)
    top_s, sum_s, top_t, sum_t, cross_term = share(far, st_zh, szh_s, szh_r)
    position = lax.broadcasted_iota(jnp.int32, (1, 2 * tok), 1)
    mask = jnp.where(position >= start_ref[m], 1.0, 0.0).astype(F32)
    scale_s, scale_t = mask / sum_s, mask / sum_t

    def grad_x():
        return mp.copy(grads.at[m], grads.at[m], gx_s, gx_r, other_chip)

    def grad_c():
        return mp.copy(grads.at[m], grads.at[m], gc_s, gc_r, other_core)

    def grad_d():
        return mp.copy(grads.at[other_chip], grads.at[other_chip], gd_s, gd_r, other_core)

    for h in range(2):
        cols = slice(h * tok, (h + 1) * tok)
        exp_s = jnp.exp(stud[h] - top_s[:, cols])
        exp_t = jnp.exp(teacher_ref[:, cols].astype(F32) - top_t[:, cols])
        grads[m, :, cols] = (exp_s * scale_s[:, cols] - exp_t * scale_t[:, cols]).astype(BF16)
    grad_x().start()
    grad_c().start()
    kl_ref[...] = mask * (cross_term / sum_t - top_t - jnp.log(sum_t) + top_s + jnp.log(sum_s))

    def owner_copy(block):
        return dp.copy(gh_out.at[block], gh_in.at[d], gh_s.at[block], gh_r.at[d], block)

    def hidden_terms(quarter):
        for h in range(2):
            block = 2 * quarter + h
            gh_out[block] = lax.dot_general(
                grads[quarter, :, h * tok : (h + 1) * tok],
                head_ref[...],
                (((0,), (0,)), ((), ())),
                preferred_element_type=F32,
            ).astype(BF16)

            @pl.when(block != d)
            def _():
                owner_copy(block).start()

    hidden_terms(m)
    grad_c().wait()
    hidden_terms(other_core)
    grad_x().wait()
    grad_d().start()
    hidden_terms(other_chip)
    grad_d().wait()
    hidden_terms(diagonal)

    scatter_wait(dp, gh_out, gh_in, gh_s, gh_r)
    gh_in[d] = gh_out[d]
    total = gh_in[0].astype(F32)
    for i in range(1, n_dp):
        total = total + gh_in[i].astype(F32)

    rows = tok // n_zl
    for i in range(n_zl):
        acc[i] = total[i * rows : (i + 1) * rows, :]
        zl_out[i] = acc[i].astype(BF16)
    scatter_start(near, zl_out, zl_in, zl_s, zl_r)
    scatter_wait(near, zl_out, zl_in, zl_s, zl_r)
    total = acc[zl]
    for peer in near.others():
        total = total + zl_in[peer].astype(F32)
    few = rows // n_zh
    for i in range(n_zh):
        zh_out[i] = total[i * few : (i + 1) * few, :].astype(BF16)
    scatter_start(far, zh_out, zh_in, zh_s, zh_r)

    def head_step(quarter, carry):
        tokens = hid[pl.ds(2 * quarter, 2)].reshape(2 * tok, depth)
        head_acc[...] += jnp.dot(grads[quarter], tokens, preferred_element_type=F32)
        return carry

    head_acc[...] = jnp.zeros_like(head_acc)
    lax.fori_loop(0, n_y, head_step, 0)
    head_out[...] = head_acc[...].astype(BF16)
    store_head = pltpu.make_async_copy(head_out, grad_head_hbm, local_sem.at[3])
    store_head.start()

    scatter_wait(far, zh_out, zh_in, zh_s, zh_r)
    zh_in[zh] = zh_out[zh]
    total = zh_in[0].astype(F32)
    for i in range(1, n_zh):
        total = total + zh_in[i].astype(F32)
    fin_h[zh] = total.astype(BF16)
    gather_start(far, fin_h.at[zh], fin_h, fh_s, fh_r)
    gather_wait(far, fin_h.at[zh], fin_h, fh_s, fh_r)
    for i in range(n_zh):
        fin_f[i * few : (i + 1) * few, :] = fin_h[i].astype(F32)
    fin_l[zl] = fin_f[...].astype(BF16)
    gather_start(near, fin_l.at[zl], fin_l, fl_s, fl_r)
    gather_wait(near, fin_l.at[zl], fin_l, fl_s, fl_r)
    for i in range(n_zl):
        grad_hidden_ref[i * rows : (i + 1) * rows, :] = fin_l[i].astype(F32)

    to_partner(d).wait_send()
    for i in range(2):
        for peer in column.others():
            to_column(2 * y + i, peer).wait_send()
    for block in [partner] + blocks_of(0) + blocks_of(1):
        for side in range(2):
            to_ring(block, side, z % 2).wait_send()
    store_head.wait()


def copy_kernel(a, b, c, a_out, b_out, c_out, sems):
    copies = [
        pltpu.make_async_copy(src, dst, sems.at[i])
        for i, (src, dst) in enumerate(((a, a_out), (b, b_out), (c, c_out)))
    ]
    for copy in copies:
        copy.start()
    for copy in copies:
        copy.wait()


def solution(mesh):
    n_dp, n_z, n_mp = mesh.shape["dp"], mesh.shape["vocab"], mesh.shape["mp"]
    n_zl = min(4, n_z)
    n_zh = n_z // n_zl

    def per_device(hidden, head_weight, teacher_logits, response_start):
        tok, depth = hidden.shape
        own, cols = teacher_logits.shape
        assert n_mp == 4 and own == 2 * tok == LEN and n_dp == 8 and n_zh == 8
        rows = tok // n_zl
        few = rows // n_zh
        dma = pltpu.SemaphoreType.DMA
        vmem = pl.BlockSpec(memory_space=pltpu.VMEM)
        hbm = pl.BlockSpec(memory_space=pl.ANY)
        shapes = (
            jax.ShapeDtypeStruct((1, own), F32),
            jax.ShapeDtypeStruct((tok, depth), F32),
            jax.ShapeDtypeStruct((cols, depth), BF16),
        )
        results = pl.pallas_call(
            functools.partial(kernel, (n_dp, n_z, n_zl, n_zh)),
            name="distill",
            out_shape=shapes,
            in_specs=[hbm, hbm, hbm, pl.BlockSpec(memory_space=pltpu.SMEM)],
            out_specs=(vmem, vmem, hbm),
            scratch_shapes=[
                pltpu.VMEM((cols, depth), BF16),
                pltpu.VMEM((cols, own), BF16),
                pltpu.VMEM((cols, depth), BF16),
                pltpu.VMEM((n_dp, 4, tok // 4, depth), BF16),
                pltpu.VMEM((4, 2, cols, tok), F32),
                pltpu.VMEM((4, cols, tok), F32),
                pltpu.VMEM((2, cols, tok), F32),
                pltpu.VMEM((2, cols, tok), F32),
                pltpu.VMEM((2, cols, tok), F32),
                pltpu.VMEM((n_dp, 8, own), F32),
                pltpu.VMEM((n_zl, 8, own), F32),
                pltpu.VMEM((n_zh, 8, own), F32),
                pltpu.VMEM((4, cols, own), BF16),
                pltpu.VMEM((n_dp, tok, depth), BF16),
                pltpu.VMEM((n_dp, tok, depth), BF16),
                pltpu.VMEM((n_zl, rows, depth), F32),
                pltpu.VMEM((n_zl, rows, depth), BF16),
                pltpu.VMEM((n_zl, rows, depth), BF16),
                pltpu.VMEM((n_zh, few, depth), BF16),
                pltpu.VMEM((n_zh, few, depth), BF16),
                pltpu.VMEM((n_zh, few, depth), BF16),
                pltpu.VMEM((rows, depth), F32),
                pltpu.VMEM((n_zl, rows, depth), BF16),
                pltpu.VMEM((cols, depth), F32),
                dma((4,)),
                pltpu.SemaphoreType.REGULAR((3,)),
                dma, dma,
                dma((2, n_dp // 2)), dma((n_dp,)),
                dma((n_dp, 2)), dma((n_dp, 2)),
                dma((4,)), dma((4,)),
                dma((2,)), dma((2,)),
                dma((n_dp,)), dma((n_dp,)),
                dma((n_zl,)), dma((n_zl,)),
                dma((n_zh,)), dma((n_zh,)),
                dma, dma,
                dma, dma,
                dma, dma,
                dma((n_dp,)), dma((n_dp,)),
                dma((n_zl,)), dma((n_zl,)),
                dma((n_zh,)), dma((n_zh,)),
                dma((n_zh,)), dma((n_zh,)),
                dma((n_zl,)), dma((n_zl,)),
            ],
            compiler_params=pltpu.CompilerParams(
                collective_id=0, has_side_effects=True, vmem_limit_bytes=56 << 20
            ),
        )(hidden.reshape(4, tok // 4, depth), head_weight.T, teacher_logits.T, response_start)
        kl, grad_hidden, grad_head = pl.pallas_call(
            copy_kernel,
            name="results",
            out_shape=shapes,
            in_specs=[hbm, hbm, hbm],
            out_specs=(hbm, hbm, hbm),
            scratch_shapes=[dma((3,))],
        )(*results)
        return kl.reshape(own), grad_hidden, grad_head.T

    return jax.shard_map(
        per_device,
        mesh=mesh,
        in_specs=(P("dp", "mp"), P("mp", ("dp", "vocab")), P("mp", ("dp", "vocab")), P()),
        out_specs=(P("mp"), P("dp", "mp"), P("mp", ("dp", "vocab"))),
        check_vma=False,
    )
```

time: 178 us -> 201 us (1.13); the launches traced: 178 us -> 199 us
  Pallas kernels: 172 us -> 198 us
  local copies, waits for them, and re-layouts: 5.34 us -> 0 us
    pallas_call x1 -> x2, Pallas kernels: 172 us -> 198 us  [the longest x1 150 us: per_device(): pl.pallas_call(functools.partial(kernel, (n_dp, n_z, n_zl, n_zh)), name='...]
    unnamed x3 -> x0, local copies, waits for them, and re-layouts: 5.34 us -> none
where the time goes in v2:
time: 201 us; the launch traced here: 199 us
  Pallas kernels  198 us (99%)
    pallas_call x1, Pallas kernels, per_device(): pl.pallas_call(functools.partial(kernel, (n_dp, n_z, n_zl, n_zh)), name='...  150 us
    pallas_call x1, Pallas kernels, per_device(): pl.pallas_call(copy_kernel, name='results', out_shape=shapes, in_specs=[h...  47.6 us

profile of v2, /device:TPU:6, one launch (start us, length us, event | category | flops | bytes accessed | tf_op | source)
XLA Modules:
  0.0 198.5 jit_solution(4338353634692738347)
XLA Ops:
  0.6 150.3 %distill.1 = (f32[1,256]{1,0:T(1,128)}, f32[128,896]{1,0:T(8,128)}, bf16[594,896]{1,0:T(8,128)(2,1)}) custom-call(bf16[4,32,896]{2,1,0:T(8,128)(2,1)} %bitcast.7, bf16[594,896]{1,0:T(8,128)(2,1)} %bitcast.5, bf16[594,256]{1,0:T(8,128)(2,1)} %bitcast.6, s32[4]{0:T(128)} %start_ref.1), custom_call_target="tpu_custom_call" | custom-call | tf_op jit(solution)/shard_map/distill/pallas_call | solution.py:397
  150.9 47.6 %results.1 = (f32[1,256]{1,0:T(1,128)}, f32[128,896]{1,0:T(8,128)}, bf16[594,896]{1,0:T(8,128)(2,1)}) custom-call(f32[1,256]{1,0:T(1,128)} %get-tuple-element.9.a, f32[128,896]{1,0:T(8,128)} %get-tuple-element.10.b, bf16[594,896]{1,0:T(8,128)(2,1)} %get-tuple-element.11.c), custom_call_target="tpu_custom_call" | custom-call | tf_op jit(solution)/shard_map/results/pallas_call | solution.py:451

commit v3 on v2

--- a/solution.py
+++ b/solution.py
@@ -249,6 +249,14 @@
         for row, value in enumerate(stats):
             st_dp[d, row : row + 1, cols] = value
 
+    to_partner(d).wait_send()
+    for i in range(2):
+        for peer in column.others():
+            to_column(2 * y + i, peer).wait_send()
+    for block in [partner] + blocks_of(0) + blocks_of(1):
+        for side in range(2):
+            to_ring(block, side, z % 2).wait_send()
+
     def share(group, held, send, recv):
         gather_start(group, held.at[group.me], held, send, recv)
         gather_wait(group, held.at[group.me], held, send, recv)
@@ -354,24 +362,19 @@
     for i in range(n_zl):
         grad_hidden_ref[i * rows : (i + 1) * rows, :] = fin_l[i].astype(F32)
 
-    to_partner(d).wait_send()
-    for i in range(2):
-        for peer in column.others():
-            to_column(2 * y + i, peer).wait_send()
-    for block in [partner] + blocks_of(0) + blocks_of(1):
-        for side in range(2):
-            to_ring(block, side, z % 2).wait_send()
     store_head.wait()
 
 
-def copy_kernel(a, b, c, a_out, b_out, c_out, sems):
-    copies = [
-        pltpu.make_async_copy(src, dst, sems.at[i])
-        for i, (src, dst) in enumerate(((a, a_out), (b, b_out), (c, c_out)))
-    ]
-    for copy in copies:
+def copy_kernel(*refs):
+    sources, results, held, (load, store) = refs[:3], refs[3:6], refs[6:9], refs[9:]
+    loads = [pltpu.make_async_copy(a, b, load.at[i]) for i, (a, b) in enumerate(zip(sources, held))]
+    stores = [pltpu.make_async_copy(a, b, store.at[i]) for i, (a, b) in enumerate(zip(held, results))]
+    for copy in loads:
         copy.start()
-    for copy in copies:
+    for before, after in zip(loads, stores):
+        before.wait()
+        after.start()
+    for copy in stores:
         copy.wait()
 
 
@@ -454,7 +457,7 @@
             out_shape=shapes,
             in_specs=[hbm, hbm, hbm],
             out_specs=(hbm, hbm, hbm),
-            scratch_shapes=[dma((3,))],
+            scratch_shapes=[pltpu.VMEM(s.shape, s.dtype) for s in shapes] + [dma((3,)), dma((3,))],
         )(*results)
         return kl.reshape(own), grad_hidden, grad_head.T
 

time: 201 us -> 156 us (0.78)
  Pallas kernels: 198 us -> 153 us
    pallas_call x1, Pallas kernels: 47.6 us -> 2.41 us  [per_device(): pl.pallas_call(copy_kernel, name='results', out_shape=shapes, in_specs=[h...]
where the time goes in v3:
time: 156 us; the launch traced here: 153 us
  Pallas kernels  153 us (98%)
    pallas_call x1, Pallas kernels, per_device(): pl.pallas_call(functools.partial(kernel, (n_dp, n_z, n_zl, n_zh)), name='...  150 us

profile of v3, /device:TPU:6, one launch (start us, length us, event | category | flops | bytes accessed | tf_op | source)
XLA Modules:
  0.0 153.3 jit_solution(14107925166911486298)
XLA Ops:
  0.6 150.3 %distill.1 = (f32[1,256]{1,0:T(1,128)}, f32[128,896]{1,0:T(8,128)}, bf16[594,896]{1,0:T(8,128)(2,1)}) custom-call(bf16[4,32,896]{2,1,0:T(8,128)(2,1)} %bitcast.7, bf16[594,896]{1,0:T(8,128)(2,1)} %bitcast.5, bf16[594,256]{1,0:T(8,128)(2,1)} %bitcast.6, s32[4]{0:T(128)} %start_ref.1), custom_call_target="tpu_custom_call" | custom-call | tf_op jit(solution)/shard_map/distill/pallas_call | solution.py:400
  150.9 2.4 %results.1 = (f32[1,256]{1,0:T(1,128)}, f32[128,896]{1,0:T(8,128)}, bf16[594,896]{1,0:T(8,128)(2,1)}) custom-call(f32[1,256]{1,0:T(1,128)} %get-tuple-element.9.refs_0_, f32[128,896]{1,0:T(8,128)} %get-tuple-element.10.refs_1_, bf16[594,896]{1,0:T(8,128)(2,1)} %get-tuple-element.11.refs_2_), custom_call_target="tpu_custom_call" | custom-call | tf_op jit(solution)/shard_map/results/pallas_call | solution.py:454

commit v4 on v3

--- a/solution.py
+++ b/solution.py
@@ -84,13 +84,13 @@
     kl_ref, grad_hidden_ref, grad_head_hbm,
     head_ref, teacher_ref, head_out,
     hid, parts, swap_in, cross_out, cross_in, stud,
-    st_dp, st_zl, st_zh, grads, gh_out, gh_in, acc,
-    zl_out, zl_in, zh_out, zh_in, fin_h, fin_f, fin_l, head_acc,
+    st_dp, st_zl, st_zh, grads, gh_out, gz_in, gh_mid, gh_in,
+    pair_out, pair_in, zh_out, zh_in, fin_h, fin_f, fin_l, head_acc,
     local_sem, ready, hx_s, hx_r, hy_s, hy_r, hz_s, hz_r,
     swap_s, swap_r, cross_s, cross_r,
     sdp_s, sdp_r, szl_s, szl_r, szh_s, szh_r,
-    gx_s, gx_r, gc_s, gc_r, gd_s, gd_r, gh_s, gh_r,
-    zl_s, zl_r, zh_s, zh_r, fh_s, fh_r, fl_s, fl_r,
+    gx_s, gx_r, gc_s, gc_r, gd_s, gd_r, gz_s, gz_r, gh_s, gh_r,
+    pair_s, pair_r, zh_s, zh_r, fh_s, fh_r, fl_s, fl_r,
 ):
     n_dp, n_z, n_zl, n_zh = sizes
     n_y = n_dp // 2
@@ -103,12 +103,14 @@
     zl, zh = z % n_zl, z // n_zl
     other_core, other_chip = 2 * x + (1 - c), 2 * (1 - x) + c
     diagonal = 2 * (1 - x) + (1 - c)
+    parity = z % 2
     up, down = lax.rem(z + 1, n_z), lax.rem(z + n_z - 1, n_z)
 
     dp = Group(n_dp, d, lambda i: (i, z, m))
     column = Group(n_y, y, lambda i: (2 * i + d % 2, z, m))
     ring = Group(n_z, z, lambda i: (d, i, m))
-    near = Group(n_zl, zl, lambda i: (d, zh * n_zl + i, m))
+    mine = 2 * (zl % 2) + zl // 2
+    near = Group(n_zl, mine, lambda i: (d, zh * n_zl + 2 * (i % 2) + i // 2, m))
     far = Group(n_zh, zh, lambda i: (d, i * n_zl + zl, m))
     mp = Group(4, m, lambda i: (d, z, i))
     far_next = [far.device(lax.rem(zh + k, n_zh)) for k in (1, n_zh - 1)]
@@ -262,7 +264,7 @@
         gather_wait(group, held.at[group.me], held, send, recv)
         return merge(held, group.n)
 
-    store_stats(st_zl.at[zl], share(dp, st_dp, sdp_s, sdp_r))
+    store_stats(st_zl.at[mine], share(dp, st_dp, sdp_s, sdp_r))
     store_stats(st_zh.at[zh], share(near, st_zl, szl_s, szl_r))
     if n_zh >= 4:
         hear(2)
@@ -271,77 +273,110 @@
     mask = jnp.where(position >= start_ref[m], 1.0, 0.0).astype(F32)
     scale_s, scale_t = mask / sum_s, mask / sum_t
 
-    def grad_x():
-        return mp.copy(grads.at[m], grads.at[m], gx_s, gx_r, other_chip)
-
-    def grad_c():
-        return mp.copy(grads.at[m], grads.at[m], gc_s, gc_r, other_core)
-
-    def grad_d():
-        return mp.copy(grads.at[other_chip], grads.at[other_chip], gd_s, gd_r, other_core)
+    def grad_x(h):
+        block = grads.at[2 * m + h]
+        return mp.copy(block, block, gx_s.at[h], gx_r.at[h], other_chip)
+
+    def grad_c(h):
+        block = grads.at[2 * m + h]
+        return mp.copy(block, block, gc_s.at[h], gc_r.at[h], other_core)
+
+    def grad_d(h):
+        block = grads.at[2 * other_chip + h]
+        return mp.copy(block, block, gd_s.at[h], gd_r.at[h], other_core)
 
     for h in range(2):
         cols = slice(h * tok, (h + 1) * tok)
         exp_s = jnp.exp(stud[h] - top_s[:, cols])
         exp_t = jnp.exp(teacher_ref[:, cols].astype(F32) - top_t[:, cols])
-        grads[m, :, cols] = (exp_s * scale_s[:, cols] - exp_t * scale_t[:, cols]).astype(BF16)
-    grad_x().start()
-    grad_c().start()
+        grads[2 * m + h] = (exp_s * scale_s[:, cols] - exp_t * scale_t[:, cols]).astype(BF16)
+        grad_x(h).start()
+        grad_c(h).start()
     kl_ref[...] = mask * (cross_term / sum_t - top_t - jnp.log(sum_t) + top_s + jnp.log(sum_s))
 
+    def to_neighbour(block, side):
+        return ring.copy(
+            gh_out.at[block, 2 * (1 - parity) + side],
+            gz_in.at[block, side],
+            gz_s.at[block, side],
+            gz_r.at[block, side],
+            (up, down)[side],
+        )
+
     def owner_copy(block):
-        return dp.copy(gh_out.at[block], gh_in.at[d], gh_s.at[block], gh_r.at[d], block)
-
-    def hidden_terms(quarter):
-        for h in range(2):
-            block = 2 * quarter + h
-            gh_out[block] = lax.dot_general(
-                grads[quarter, :, h * tok : (h + 1) * tok],
-                head_ref[...],
-                (((0,), (0,)), ((), ())),
-                preferred_element_type=F32,
-            ).astype(BF16)
-
-            @pl.when(block != d)
-            def _():
-                owner_copy(block).start()
-
-    hidden_terms(m)
-    grad_c().wait()
-    hidden_terms(other_core)
-    grad_x().wait()
-    grad_d().start()
-    hidden_terms(other_chip)
-    grad_d().wait()
-    hidden_terms(diagonal)
-
-    scatter_wait(dp, gh_out, gh_in, gh_s, gh_r)
-    gh_in[d] = gh_out[d]
-    total = gh_in[0].astype(F32)
-    for i in range(1, n_dp):
-        total = total + gh_in[i].astype(F32)
-
+        return dp.copy(gh_mid.at[block], gh_in.at[d], gh_s.at[block], gh_r.at[d], block)
+
+    def hidden_terms(block):
+        gh_out[block] = (
+            lax.dot_general(
+                grads[block], head_ref[...], (((0,), (0,)), ((), ())), preferred_element_type=F32
+            )
+            .astype(BF16)
+            .reshape(4, sub, depth)
+        )
+        for side in range(2):
+            to_neighbour(block, side).start()
+
+    def hand_over(block):
+        for side in range(2):
+            to_neighbour(block, side).wait()
+            own_rows = gh_out[block, 2 * parity + side].astype(F32)
+            gh_mid[block, side] = (own_rows + gz_in[block, side].astype(F32)).astype(BF16)
+
+        @pl.when(block != d)
+        def _():
+            owner_copy(block).start()
+
+    for h in range(2):
+        hidden_terms(2 * m + h)
+    for h in range(2):
+        grad_c(h).wait()
+        hidden_terms(2 * other_core + h)
+    for h in range(2):
+        hand_over(2 * m + h)
+    for h in range(2):
+        grad_x(h).wait()
+        grad_d(h).start()
+        hidden_terms(2 * other_chip + h)
+        hand_over(2 * other_core + h)
+    for h in range(2):
+        grad_d(h).wait()
+        hidden_terms(2 * diagonal + h)
+    for h in range(2):
+        hand_over(2 * other_chip + h)
+    for h in range(2):
+        hand_over(2 * diagonal + h)
+
+    scatter_wait(dp, gh_mid, gh_in, gh_s, gh_r)
+    gh_in[d] = gh_mid[d]
     rows = tok // n_zl
-    for i in range(n_zl):
-        acc[i] = total[i * rows : (i + 1) * rows, :]
-        zl_out[i] = acc[i].astype(BF16)
-    scatter_start(near, zl_out, zl_in, zl_s, zl_r)
-    scatter_wait(near, zl_out, zl_in, zl_s, zl_r)
-    total = acc[zl]
-    for peer in near.others():
-        total = total + zl_in[peer].astype(F32)
+
+    def pair_copy():
+        return near.copy(pair_out, pair_in, pair_s, pair_r, 2 * (mine // 2) + 1 - mine % 2)
+
+    def plane_sum(side):
+        total = gh_in[0, side].astype(F32)
+        for i in range(1, n_dp):
+            total = total + gh_in[i, side].astype(F32)
+        return total
+
+    pair_out[...] = plane_sum(1 - mine % 2).astype(BF16)
+    pair_copy().start()
+    total = plane_sum(mine % 2)
+    pair_copy().wait()
+    total = total + pair_in[...].astype(F32)
     few = rows // n_zh
     for i in range(n_zh):
         zh_out[i] = total[i * few : (i + 1) * few, :].astype(BF16)
     scatter_start(far, zh_out, zh_in, zh_s, zh_r)
 
-    def head_step(quarter, carry):
-        tokens = hid[pl.ds(2 * quarter, 2)].reshape(2 * tok, depth)
-        head_acc[...] += jnp.dot(grads[quarter], tokens, preferred_element_type=F32)
+    def head_step(block, carry):
+        tokens = hid[block].reshape(tok, depth)
+        head_acc[...] += jnp.dot(grads[block], tokens, preferred_element_type=F32)
         return carry
 
     head_acc[...] = jnp.zeros_like(head_acc)
-    lax.fori_loop(0, n_y, head_step, 0)
+    lax.fori_loop(0, n_dp, head_step, 0)
     head_out[...] = head_acc[...].astype(BF16)
     store_head = pltpu.make_async_copy(head_out, grad_head_hbm, local_sem.at[3])
     store_head.start()
@@ -356,9 +391,9 @@
     gather_wait(far, fin_h.at[zh], fin_h, fh_s, fh_r)
     for i in range(n_zh):
         fin_f[i * few : (i + 1) * few, :] = fin_h[i].astype(F32)
-    fin_l[zl] = fin_f[...].astype(BF16)
-    gather_start(near, fin_l.at[zl], fin_l, fl_s, fl_r)
-    gather_wait(near, fin_l.at[zl], fin_l, fl_s, fl_r)
+    fin_l[mine] = fin_f[...].astype(BF16)
+    gather_start(near, fin_l.at[mine], fin_l, fl_s, fl_r)
+    gather_wait(near, fin_l.at[mine], fin_l, fl_s, fl_r)
     for i in range(n_zl):
         grad_hidden_ref[i * rows : (i + 1) * rows, :] = fin_l[i].astype(F32)
 
@@ -386,7 +421,7 @@
     def per_device(hidden, head_weight, teacher_logits, response_start):
         tok, depth = hidden.shape
         own, cols = teacher_logits.shape
-        assert n_mp == 4 and own == 2 * tok == LEN and n_dp == 8 and n_zh == 8
+        assert n_mp == 4 and own == 2 * tok == LEN and n_dp == 8 and n_zl == 4 and n_zh == 8
         rows = tok // n_zl
         few = rows // n_zh
         dma = pltpu.SemaphoreType.DMA
@@ -416,12 +451,13 @@
                 pltpu.VMEM((n_dp, 8, own), F32),
                 pltpu.VMEM((n_zl, 8, own), F32),
                 pltpu.VMEM((n_zh, 8, own), F32),
-                pltpu.VMEM((4, cols, own), BF16),
-                pltpu.VMEM((n_dp, tok, depth), BF16),
-                pltpu.VMEM((n_dp, tok, depth), BF16),
-                pltpu.VMEM((n_zl, rows, depth), F32),
-                pltpu.VMEM((n_zl, rows, depth), BF16),
-                pltpu.VMEM((n_zl, rows, depth), BF16),
+                pltpu.VMEM((n_dp, cols, tok), BF16),
+                pltpu.VMEM((n_dp, 4, tok // 4, depth), BF16),
+                pltpu.VMEM((n_dp, 2, tok // 4, depth), BF16),
+                pltpu.VMEM((n_dp, 2, tok // 4, depth), BF16),
+                pltpu.VMEM((n_dp, 2, tok // 4, depth), BF16),
+                pltpu.VMEM((rows, depth), BF16),
+                pltpu.VMEM((rows, depth), BF16),
                 pltpu.VMEM((n_zh, few, depth), BF16),
                 pltpu.VMEM((n_zh, few, depth), BF16),
                 pltpu.VMEM((n_zh, few, depth), BF16),
@@ -438,11 +474,12 @@
                 dma((n_dp,)), dma((n_dp,)),
                 dma((n_zl,)), dma((n_zl,)),
                 dma((n_zh,)), dma((n_zh,)),
+                dma((2,)), dma((2,)),
+                dma((2,)), dma((2,)),
+                dma((2,)), dma((2,)),
+                dma((n_dp, 2)), dma((n_dp, 2)),
+                dma((n_dp,)), dma((n_dp,)),
                 dma, dma,
-                dma, dma,
-                dma, dma,
-                dma((n_dp,)), dma((n_dp,)),
-                dma((n_zl,)), dma((n_zl,)),
                 dma((n_zh,)), dma((n_zh,)),
                 dma((n_zh,)), dma((n_zh,)),
                 dma((n_zl,)), dma((n_zl,)),

time: 156 us -> 146 us (0.936)
  Pallas kernels: 153 us -> 143 us
    pallas_call x1, Pallas kernels: 150 us -> 140 us  [per_device(): pl.pallas_call(functools.partial(kernel, (n_dp, n_z, n_zl, n_zh)), name='...]
where the time goes in v4:
time: 146 us; the launch traced here: 143 us
  Pallas kernels  143 us (98%)
    pallas_call x1, Pallas kernels, per_device(): pl.pallas_call(functools.partial(kernel, (n_dp, n_z, n_zl, n_zh)), name='...  140 us

profile of v4, /device:TPU:6, one launch (start us, length us, event | category | flops | bytes accessed | tf_op | source)
XLA Modules:
  0.0 143.2 jit_solution(230807258625113313)
XLA Ops:
  0.6 140.1 %distill.1 = (f32[1,256]{1,0:T(1,128)}, f32[128,896]{1,0:T(8,128)}, bf16[594,896]{1,0:T(8,128)(2,1)}) custom-call(bf16[4,32,896]{2,1,0:T(8,128)(2,1)} %bitcast.7, bf16[594,896]{1,0:T(8,128)(2,1)} %bitcast.5, bf16[594,256]{1,0:T(8,128)(2,1)} %bitcast.6, s32[4]{0:T(128)} %start_ref.1), custom_call_target="tpu_custom_call" | custom-call | tf_op jit(solution)/shard_map/distill/pallas_call | solution.py:435
  140.7 2.4 %results.1 = (f32[1,256]{1,0:T(1,128)}, f32[128,896]{1,0:T(8,128)}, bf16[594,896]{1,0:T(8,128)(2,1)}) custom-call(f32[1,256]{1,0:T(1,128)} %get-tuple-element.9.refs_0_, f32[128,896]{1,0:T(8,128)} %get-tuple-element.10.refs_1_, bf16[594,896]{1,0:T(8,128)(2,1)} %get-tuple-element.11.refs_2_), custom_call_target="tpu_custom_call" | custom-call | tf_op jit(solution)/shard_map/results/pallas_call | solution.py:491

commit v5 on v4

--- a/solution.py
+++ b/solution.py
@@ -20,7 +20,8 @@
         self.n, self.me, self.device = n, me, device
 
     def others(self):
-        return [lax.rem(self.me + k, self.n) for k in range(1, self.n)]
+        shifts = sorted(range(1, self.n), key=lambda k: -min(k, self.n - k))
+        return [lax.rem(self.me + k, self.n) for k in shifts]
 
     def copy(self, src, dst, send, recv, to):
         return pltpu.make_async_remote_copy(
@@ -85,12 +86,12 @@
     head_ref, teacher_ref, head_out,
     hid, parts, swap_in, cross_out, cross_in, stud,
     st_dp, st_zl, st_zh, grads, gh_out, gz_in, gh_mid, gh_in,
-    pair_out, pair_in, zh_out, zh_in, fin_h, fin_f, fin_l, head_acc,
+    zs_out, zs_in, fin, fin_other, head_acc,
     local_sem, ready, hx_s, hx_r, hy_s, hy_r, hz_s, hz_r,
     swap_s, swap_r, cross_s, cross_r,
     sdp_s, sdp_r, szl_s, szl_r, szh_s, szh_r,
     gx_s, gx_r, gc_s, gc_r, gd_s, gd_r, gz_s, gz_r, gh_s, gh_r,
-    pair_s, pair_r, zh_s, zh_r, fh_s, fh_r, fl_s, fl_r,
+    zs_s, zs_r, fa_s, fa_r, fo_s, fo_r,
 ):
     n_dp, n_z, n_zl, n_zh = sizes
     n_y = n_dp // 2
@@ -111,6 +112,7 @@
     ring = Group(n_z, z, lambda i: (d, i, m))
     mine = 2 * (zl % 2) + zl // 2
     near = Group(n_zl, mine, lambda i: (d, zh * n_zl + 2 * (i % 2) + i // 2, m))
+    alike = Group(n_z // 2, z // 2, lambda i: (d, 2 * i + parity, m))
     far = Group(n_zh, zh, lambda i: (d, i * n_zl + zl, m))
     mp = Group(4, m, lambda i: (d, z, i))
     far_next = [far.device(lax.rem(zh + k, n_zh)) for k in (1, n_zh - 1)]
@@ -118,6 +120,7 @@
     barrier = pltpu.get_barrier_semaphore()
     peers = [g.device(p) for g in (dp, near) for p in g.others()] + far_next
     peers += [mp.device(other_core), mp.device(other_chip), ring.device(up), ring.device(down)]
+    peers += [ring.device(lax.rem(z + k, n_z)) for k in (2, n_z - 2)]
     for peer in peers:
         pl.semaphore_signal(barrier, inc=1, device_id=peer, device_id_type=MESH)
     own = pltpu.make_async_copy(hidden_ref, hid.at[d], local_sem.at[0])
@@ -169,7 +172,7 @@
         tell(0)
 
     def blocks_of(i):
-        return [2 * row + i for row in column.others()]
+        return [2 * row + i for row in reversed(column.others())]
 
     def forward(i):
         for block in blocks_of(i):
@@ -349,26 +352,15 @@
 
     scatter_wait(dp, gh_mid, gh_in, gh_s, gh_r)
     gh_in[d] = gh_mid[d]
-    rows = tok // n_zl
-
-    def pair_copy():
-        return near.copy(pair_out, pair_in, pair_s, pair_r, 2 * (mine // 2) + 1 - mine % 2)
-
-    def plane_sum(side):
+    few = tok // n_z
+    each = sub // few
+    for side in range(2):
         total = gh_in[0, side].astype(F32)
         for i in range(1, n_dp):
             total = total + gh_in[i, side].astype(F32)
-        return total
-
-    pair_out[...] = plane_sum(1 - mine % 2).astype(BF16)
-    pair_copy().start()
-    total = plane_sum(mine % 2)
-    pair_copy().wait()
-    total = total + pair_in[...].astype(F32)
-    few = rows // n_zh
-    for i in range(n_zh):
-        zh_out[i] = total[i * few : (i + 1) * few, :].astype(BF16)
-    scatter_start(far, zh_out, zh_in, zh_s, zh_r)
+        for i in range(each):
+            zs_out[side * each + i] = total[i * few : (i + 1) * few, :].astype(BF16)
+    scatter_start(alike, zs_out, zs_in, zs_s, zs_r)
 
     def head_step(block, carry):
         tokens = hid[block].reshape(tok, depth)
@@ -381,22 +373,36 @@
     store_head = pltpu.make_async_copy(head_out, grad_head_hbm, local_sem.at[3])
     store_head.start()
 
-    scatter_wait(far, zh_out, zh_in, zh_s, zh_r)
-    zh_in[zh] = zh_out[zh]
-    total = zh_in[0].astype(F32)
-    for i in range(1, n_zh):
-        total = total + zh_in[i].astype(F32)
-    fin_h[zh] = total.astype(BF16)
-    gather_start(far, fin_h.at[zh], fin_h, fh_s, fh_r)
-    gather_wait(far, fin_h.at[zh], fin_h, fh_s, fh_r)
-    for i in range(n_zh):
-        fin_f[i * few : (i + 1) * few, :] = fin_h[i].astype(F32)
-    fin_l[mine] = fin_f[...].astype(BF16)
-    gather_start(near, fin_l.at[mine], fin_l, fl_s, fl_r)
-    gather_wait(near, fin_l.at[mine], fin_l, fl_s, fl_r)
-    for i in range(n_zl):
-        grad_hidden_ref[i * rows : (i + 1) * rows, :] = fin_l[i].astype(F32)
-
+    scatter_wait(alike, zs_out, zs_in, zs_s, zs_r)
+    me = alike.me
+    zs_in[me] = zs_out[me]
+    total = zs_in[0].astype(F32)
+    for i in range(1, alike.n):
+        total = total + zs_in[i].astype(F32)
+    fin[me] = total.astype(BF16)
+    gather_start(alike, fin.at[me], fin, fa_s, fa_r)
+    gather_wait(alike, fin.at[me], fin, fa_s, fa_r)
+
+    def exchange(side):
+        return ring.copy(
+            fin.at[pl.ds(side * each, each)],
+            fin_other.at[side],
+            fo_s.at[side],
+            fo_r.at[side],
+            (up, down)[side],
+        )
+
+    for side in range(2):
+        exchange(side).start()
+    for side in range(2):
+        for i in range(each):
+            rows = slice(i * few, (i + 1) * few)
+            grad_hidden_ref[2 * parity + side, rows, :] = fin[side * each + i].astype(F32)
+    for side in range(2):
+        exchange(side).wait()
+        for i in range(each):
+            rows = slice(i * few, (i + 1) * few)
+            grad_hidden_ref[2 * (1 - parity) + side, rows, :] = fin_other[side, i].astype(F32)
     store_head.wait()
 
 
@@ -422,14 +428,13 @@
         tok, depth = hidden.shape
         own, cols = teacher_logits.shape
         assert n_mp == 4 and own == 2 * tok == LEN and n_dp == 8 and n_zl == 4 and n_zh == 8
-        rows = tok // n_zl
-        few = rows // n_zh
+        few = tok // n_z
         dma = pltpu.SemaphoreType.DMA
         vmem = pl.BlockSpec(memory_space=pltpu.VMEM)
         hbm = pl.BlockSpec(memory_space=pl.ANY)
         shapes = (
             jax.ShapeDtypeStruct((1, own), F32),
-            jax.ShapeDtypeStruct((tok, depth), F32),
+            jax.ShapeDtypeStruct((4, tok // 4, depth), F32),
             jax.ShapeDtypeStruct((cols, depth), BF16),
         )
         results = pl.pallas_call(
@@ -456,13 +461,10 @@
                 pltpu.VMEM((n_dp, 2, tok // 4, depth), BF16),
                 pltpu.VMEM((n_dp, 2, tok // 4, depth), BF16),
                 pltpu.VMEM((n_dp, 2, tok // 4, depth), BF16),
-                pltpu.VMEM((rows, depth), BF16),
-                pltpu.VMEM((rows, depth), BF16),
-                pltpu.VMEM((n_zh, few, depth), BF16),
-                pltpu.VMEM((n_zh, few, depth), BF16),
-                pltpu.VMEM((n_zh, few, depth), BF16),
-                pltpu.VMEM((rows, depth), F32),
-                pltpu.VMEM((n_zl, rows, depth), BF16),
+                pltpu.VMEM((n_z // 2, few, depth), BF16),
+                pltpu.VMEM((n_z // 2, few, depth), BF16),
+                pltpu.VMEM((n_z // 2, few, depth), BF16),
+                pltpu.VMEM((2, n_z // 4, few, depth), BF16),
                 pltpu.VMEM((cols, depth), F32),
                 dma((4,)),
                 pltpu.SemaphoreType.REGULAR((3,)),
@@ -479,10 +481,9 @@
                 dma((2,)), dma((2,)),
                 dma((n_dp, 2)), dma((n_dp, 2)),
                 dma((n_dp,)), dma((n_dp,)),
-                dma, dma,
-                dma((n_zh,)), dma((n_zh,)),
-                dma((n_zh,)), dma((n_zh,)),
-                dma((n_zl,)), dma((n_zl,)),
+                dma((n_z // 2,)), dma((n_z // 2,)),
+                dma((n_z // 2,)), dma((n_z // 2,)),
+                dma((2,)), dma((2,)),
             ],
             compiler_params=pltpu.CompilerParams(
                 collective_id=0, has_side_effects=True, vmem_limit_bytes=56 << 20
@@ -496,7 +497,7 @@
             out_specs=(hbm, hbm, hbm),
             scratch_shapes=[pltpu.VMEM(s.shape, s.dtype) for s in shapes] + [dma((3,)), dma((3,))],
         )(*results)
-        return kl.reshape(own), grad_hidden, grad_head.T
+        return kl.reshape(own), grad_hidden.reshape(tok, depth), grad_head.T
 
     return jax.shard_map(
         per_device,

time: 146 us -> 144 us (0.986); the launches traced: 143 us -> 144 us
  no operation moved by 1% of the time
where the time goes in v5:
time: 144 us
  Pallas kernels  143 us (99%)
    pallas_call x1, Pallas kernels, per_device(): pl.pallas_call(functools.partial(kernel, (n_dp, n_z, n_zl, n_zh)), name='...  141 us

profile of v5, /device:TPU:6, one launch (start us, length us, event | category | flops | bytes accessed | tf_op | source)
XLA Modules:
  0.0 143.7 jit_solution(7395374737590727416)
XLA Ops:
  0.6 140.6 %distill.1 = (f32[1,256]{1,0:T(1,128)}, f32[4,32,896]{2,1,0:T(8,128)}, bf16[594,896]{1,0:T(8,128)(2,1)}) custom-call(bf16[4,32,896]{2,1,0:T(8,128)(2,1)} %bitcast.8, bf16[594,896]{1,0:T(8,128)(2,1)} %bitcast.6, bf16[594,256]{1,0:T(8,128)(2,1)} %bitcast.7, s32[4]{0:T(128)} %start_ref.1), custom_call_target="tpu_custom_call" | custom-call | tf_op jit(solution)/shard_map/distill/pallas_call | solution.py:440
  141.2 2.4 %results.1 = (f32[1,256]{1,0:T(1,128)}, f32[4,32,896]{2,1,0:T(8,128)}, bf16[594,896]{1,0:T(8,128)(2,1)}) custom-call(f32[1,256]{1,0:T(1,128)} %get-tuple-element.9.refs_0_, f32[4,32,896]{2,1,0:T(8,128)} %get-tuple-element.10.refs_1_, bf16[594,896]{1,0:T(8,128)(2,1)} %get-tuple-element.11.refs_2_), custom_call_target="tpu_custom_call" | custom-call | tf_op jit(solution)/shard_map/results/pallas_call | solution.py:492

commit v6 on v5

--- a/solution.py
+++ b/solution.py
@@ -83,14 +83,14 @@
     sizes,
     hidden_ref, head_hbm, teacher_hbm, start_ref,
     kl_ref, grad_hidden_ref, grad_head_hbm,
-    head_ref, teacher_ref, head_out,
-    hid, parts, swap_in, cross_out, cross_in, stud,
+    head_ref, teacher_ref, head_out, student_exp, scales,
+    hid, parts, swap_in, cross_out, cross_in,
     st_dp, st_zl, st_zh, grads, gh_out, gz_in, gh_mid, gh_in,
     zs_out, zs_in, fin, fin_other, head_acc,
-    local_sem, ready, hx_s, hx_r, hy_s, hy_r, hz_s, hz_r,
+    local_sem, teacher_sem, ready, hx_s, hx_r, hy_s, hy_r, hz_s, hz_r,
     swap_s, swap_r, cross_s, cross_r,
     sdp_s, sdp_r, szl_s, szl_r, szh_s, szh_r,
-    gx_s, gx_r, gc_s, gc_r, gd_s, gd_r, gz_s, gz_r, gh_s, gh_r,
+    t_s, t_r, e_s, e_r, sc_s, sc_r, gz_s, gz_r, gh_s, gh_r,
     zs_s, zs_r, fa_s, fa_r, fo_s, fo_r,
 ):
     n_dp, n_z, n_zl, n_zh = sizes
@@ -119,7 +119,7 @@
 
     barrier = pltpu.get_barrier_semaphore()
     peers = [g.device(p) for g in (dp, near) for p in g.others()] + far_next
-    peers += [mp.device(other_core), mp.device(other_chip), ring.device(up), ring.device(down)]
+    peers += [mp.device(p) for p in mp.others()] + [ring.device(up), ring.device(down)]
     peers += [ring.device(lax.rem(z + k, n_z)) for k in (2, n_z - 2)]
     for peer in peers:
         pl.semaphore_signal(barrier, inc=1, device_id=peer, device_id_type=MESH)
@@ -127,8 +127,14 @@
     own.start()
     load_head = pltpu.make_async_copy(head_hbm, head_ref, local_sem.at[1])
     load_head.start()
-    load_teacher = pltpu.make_async_copy(teacher_hbm, teacher_ref, local_sem.at[2])
-    load_teacher.start()
+    load_teacher = [
+        pltpu.make_async_copy(
+            teacher_hbm.at[:, pl.ds(h * tok, tok)], teacher_ref.at[2 * m + h], teacher_sem.at[h]
+        )
+        for h in range(2)
+    ]
+    for load in load_teacher:
+        load.start()
     own.wait()
     pl.semaphore_wait(barrier, len(peers))
 
@@ -156,6 +162,40 @@
     def pass_on(block):
         for side in range(2):
             to_ring(block, side, z % 2).start()
+
+    class Spread:
+        def __init__(self, held, send, recv):
+            self.held, self.send, self.recv = held, send, recv
+
+        def hop(self, way, block, h, to):
+            part = self.held.at[block]
+            return mp.copy(part, part, self.send.at[way, h], self.recv.at[way, h], to)
+
+        def chip(self, h):
+            return self.hop(0, 2 * m + h, h, other_chip)
+
+        def core(self, h):
+            return self.hop(1, 2 * m + h, h, other_core)
+
+        def onward(self, h):
+            return self.hop(2, 2 * other_chip + h, h, other_core)
+
+        def start(self):
+            for h in range(2):
+                self.chip(h).start()
+                self.core(h).start()
+
+        def turn(self, h):
+            self.chip(h).wait()
+            self.onward(h).start()
+
+        def finish(self):
+            for h in range(2):
+                self.core(h).wait()
+                self.onward(h).wait()
+
+    teacher = Spread(teacher_ref, t_s, t_r)
+    student = Spread(student_exp, e_s, e_r)
 
     to_partner(d).start()
     for i in range(2):
@@ -170,6 +210,9 @@
     pass_on(partner)
     if n_zh >= 4:
         tell(0)
+    for load in load_teacher:
+        load.wait()
+    teacher.start()
 
     def blocks_of(i):
         return [2 * row + i for row in reversed(column.others())]
@@ -231,22 +274,23 @@
         tell(2)
     partial_sums(2)
     partial_sums(3)
-    load_teacher.wait()
+    for h in range(2):
+        teacher.turn(h)
 
     for h in range(2):
         cols = slice(h * tok, (h + 1) * tok)
         swap(2 + h).wait()
-        stud[h] = parts[2 + h, 1] + swap_in[2 + h]
         cross(h).wait()
-        s = stud[h] + cross_in[h]
-        stud[h] = s
-        t = teacher_ref[:, cols].astype(F32)
+        s = parts[2 + h, 1] + swap_in[2 + h] + cross_in[h]
+        t = teacher_ref[2 * m + h].astype(F32)
         top_s = jnp.max(s, axis=0, keepdims=True)
         top_t = jnp.max(t, axis=0, keepdims=True)
+        exp_s = jnp.exp(s - top_s)
         exp_t = jnp.exp(t - top_t)
+        student_exp[2 * m + h] = exp_s.astype(BF16)
         stats = (
             top_s,
-            jnp.sum(jnp.exp(s - top_s), axis=0, keepdims=True),
+            jnp.sum(exp_s, axis=0, keepdims=True),
             top_t,
             jnp.sum(exp_t, axis=0, keepdims=True),
             jnp.sum(exp_t * (t - s), axis=0, keepdims=True),
@@ -262,40 +306,40 @@
         for side in range(2):
             to_ring(block, side, z % 2).wait_send()
 
-    def share(group, held, send, recv):
+    def share(group, held, send, recv, between=None):
         gather_start(group, held.at[group.me], held, send, recv)
+        if between is not None:
+            between()
         gather_wait(group, held.at[group.me], held, send, recv)
         return merge(held, group.n)
 
+    def turns():
+        for h in range(2):
+            student.turn(h)
+        teacher.finish()
+
+    own_top_s = st_dp[d, ROW_MS : ROW_MS + 1, :]
     store_stats(st_zl.at[mine], share(dp, st_dp, sdp_s, sdp_r))
+    student.start()
     store_stats(st_zh.at[zh], share(near, st_zl, szl_s, szl_r))
     if n_zh >= 4:
         hear(2)
-    top_s, sum_s, top_t, sum_t, cross_term = share(far, st_zh, szh_s, szh_r)
+    top_s, sum_s, top_t, sum_t, cross_term = share(far, st_zh, szh_s, szh_r, turns)
     position = lax.broadcasted_iota(jnp.int32, (1, 2 * tok), 1)
     mask = jnp.where(position >= start_ref[m], 1.0, 0.0).astype(F32)
-    scale_s, scale_t = mask / sum_s, mask / sum_t
-
-    def grad_x(h):
-        block = grads.at[2 * m + h]
-        return mp.copy(block, block, gx_s.at[h], gx_r.at[h], other_chip)
-
-    def grad_c(h):
-        block = grads.at[2 * m + h]
-        return mp.copy(block, block, gc_s.at[h], gc_r.at[h], other_core)
-
-    def grad_d(h):
-        block = grads.at[2 * other_chip + h]
-        return mp.copy(block, block, gd_s.at[h], gd_r.at[h], other_core)
-
-    for h in range(2):
+    scales[m, 0:1, :] = mask * jnp.exp(own_top_s - top_s) / sum_s
+    scales[m, 1:2, :] = mask / sum_t
+    scales[m, 2:3, :] = top_t
+    gather_start(mp, scales.at[m], scales, sc_s, sc_r)
+    kl_ref[...] = mask * (cross_term / sum_t - top_t - jnp.log(sum_t) + top_s + jnp.log(sum_s))
+
+    def logit_grads(quarter, h):
         cols = slice(h * tok, (h + 1) * tok)
-        exp_s = jnp.exp(stud[h] - top_s[:, cols])
-        exp_t = jnp.exp(teacher_ref[:, cols].astype(F32) - top_t[:, cols])
-        grads[2 * m + h] = (exp_s * scale_s[:, cols] - exp_t * scale_t[:, cols]).astype(BF16)
-        grad_x(h).start()
-        grad_c(h).start()
-    kl_ref[...] = mask * (cross_term / sum_t - top_t - jnp.log(sum_t) + top_s + jnp.log(sum_s))
+        block = 2 * quarter + h
+        exp_t = jnp.exp(teacher_ref[block].astype(F32) - scales[quarter, 2:3, cols])
+        grads[block] = (
+            student_exp[block].astype(F32) * scales[quarter, 0:1, cols] - exp_t * scales[quarter, 1:2, cols]
+        ).astype(BF16)
 
     def to_neighbour(block, side):
         return ring.copy(
@@ -309,7 +353,9 @@
     def owner_copy(block):
         return dp.copy(gh_mid.at[block], gh_in.at[d], gh_s.at[block], gh_r.at[d], block)
 
-    def hidden_terms(block):
+    def hidden_terms(quarter, h):
+        logit_grads(quarter, h)
+        block = 2 * quarter + h
         gh_out[block] = (
             lax.dot_general(
                 grads[block], head_ref[...], (((0,), (0,)), ((), ())), preferred_element_type=F32
@@ -331,22 +377,14 @@
             owner_copy(block).start()
 
     for h in range(2):
-        hidden_terms(2 * m + h)
-    for h in range(2):
-        grad_c(h).wait()
-        hidden_terms(2 * other_core + h)
-    for h in range(2):
-        hand_over(2 * m + h)
-    for h in range(2):
-        grad_x(h).wait()
-        grad_d(h).start()
-        hidden_terms(2 * other_chip + h)
-        hand_over(2 * other_core + h)
-    for h in range(2):
-        grad_d(h).wait()
-        hidden_terms(2 * diagonal + h)
-    for h in range(2):
-        hand_over(2 * other_chip + h)
+        hidden_terms(m, h)
+    student.finish()
+    gather_wait(mp, scales.at[m], scales, sc_s, sc_r)
+    order = (m, other_core, other_chip, diagonal)
+    for i in range(1, 4):
+        for h in range(2):
+            hidden_terms(order[i], h)
+            hand_over(2 * order[i - 1] + h)
     for h in range(2):
         hand_over(2 * diagonal + h)
 
@@ -445,12 +483,13 @@
             out_specs=(vmem, vmem, hbm),
             scratch_shapes=[
                 pltpu.VMEM((cols, depth), BF16),
-                pltpu.VMEM((cols, own), BF16),
+                pltpu.VMEM((n_dp, cols, tok), BF16),
                 pltpu.VMEM((cols, depth), BF16),
+                pltpu.VMEM((n_dp, cols, tok), BF16),
+                pltpu.VMEM((4, 8, own), F32),
                 pltpu.VMEM((n_dp, 4, tok // 4, depth), BF16),
                 pltpu.VMEM((4, 2, cols, tok), F32),
                 pltpu.VMEM((4, cols, tok), F32),
-                pltpu.VMEM((2, cols, tok), F32),
                 pltpu.VMEM((2, cols, tok), F32),
                 pltpu.VMEM((2, cols, tok), F32),
                 pltpu.VMEM((n_dp, 8, own), F32),
@@ -467,6 +506,7 @@
                 pltpu.VMEM((2, n_z // 4, few, depth), BF16),
                 pltpu.VMEM((cols, depth), F32),
                 dma((4,)),
+                dma((2,)),
                 pltpu.SemaphoreType.REGULAR((3,)),
                 dma, dma,
                 dma((2, n_dp // 2)), dma((n_dp,)),
@@ -476,9 +516,9 @@
                 dma((n_dp,)), dma((n_dp,)),
                 dma((n_zl,)), dma((n_zl,)),
                 dma((n_zh,)), dma((n_zh,)),
-                dma((2,)), dma((2,)),
-                dma((2,)), dma((2,)),
-                dma((2,)), dma((2,)),
+                dma((3, 2)), dma((3, 2)),
+                dma((3, 2)), dma((3, 2)),
+                dma((4,)), dma((4,)),
                 dma((n_dp, 2)), dma((n_dp, 2)),
                 dma((n_dp,)), dma((n_dp,)),
                 dma((n_z // 2,)), dma((n_z // 2,)),

time: 144 us -> 143 us (level)
    pallas_call x1, Pallas kernels: 141 us -> 139 us  [per_device(): pl.pallas_call(functools.partial(kernel, (n_dp, n_z, n_zl, n_zh)), name='...]
where the time goes in v6:
time: 143 us; the launch traced here: 142 us
  Pallas kernels  142 us (99%)
    pallas_call x1, Pallas kernels, per_device(): pl.pallas_call(functools.partial(kernel, (n_dp, n_z, n_zl, n_zh)), name='...  139 us

profile of v6, /device:TPU:6, one launch (start us, length us, event | category | flops | bytes accessed | tf_op | source)
XLA Modules:
  0.0 142.2 jit_solution(8853394125957427932)
XLA Ops:
  0.6 139.1 %distill.1 = (f32[1,256]{1,0:T(1,128)}, f32[4,32,896]{2,1,0:T(8,128)}, bf16[594,896]{1,0:T(8,128)(2,1)}) custom-call(bf16[4,32,896]{2,1,0:T(8,128)(2,1)} %bitcast.8, bf16[594,896]{1,0:T(8,128)(2,1)} %bitcast.6, bf16[594,256]{1,0:T(8,128)(2,1)} %bitcast.7, s32[4]{0:T(128)} %start_ref.1), custom_call_target="tpu_custom_call" | custom-call | tf_op jit(solution)/shard_map/distill/pallas_call | solution.py:478
  139.7 2.4 %results.1 = (f32[1,256]{1,0:T(1,128)}, f32[4,32,896]{2,1,0:T(8,128)}, bf16[594,896]{1,0:T(8,128)(2,1)}) custom-call(f32[1,256]{1,0:T(1,128)} %get-tuple-element.9.refs_0_, f32[4,32,896]{2,1,0:T(8,128)} %get-tuple-element.10.refs_1_, bf16[594,896]{1,0:T(8,128)(2,1)} %get-tuple-element.11.refs_2_), custom_call_target="tpu_custom_call" | custom-call | tf_op jit(solution)/shard_map/results/pallas_call | solution.py:532

commit v7 on v6

--- a/solution.py
+++ b/solution.py
@@ -261,11 +261,11 @@
     load_head.wait()
     arrive(0)
     partial_sums(0)
+    forward(1)
     send_cross(0)
     if n_zh >= 4:
         hear(0)
         tell(1)
-    forward(1)
     arrive(1)
     partial_sums(1)
     send_cross(1)
@@ -327,19 +327,17 @@
     top_s, sum_s, top_t, sum_t, cross_term = share(far, st_zh, szh_s, szh_r, turns)
     position = lax.broadcasted_iota(jnp.int32, (1, 2 * tok), 1)
     mask = jnp.where(position >= start_ref[m], 1.0, 0.0).astype(F32)
-    scales[m, 0:1, :] = mask * jnp.exp(own_top_s - top_s) / sum_s
-    scales[m, 1:2, :] = mask / sum_t
-    scales[m, 2:3, :] = top_t
+    token_scales = mask * jnp.exp(own_top_s - top_s) / sum_s, mask / sum_t, top_t
+    for h in range(2):
+        for row, value in enumerate(token_scales):
+            scales[m, h, row : row + 1, :] = value[:, h * tok : (h + 1) * tok]
     gather_start(mp, scales.at[m], scales, sc_s, sc_r)
     kl_ref[...] = mask * (cross_term / sum_t - top_t - jnp.log(sum_t) + top_s + jnp.log(sum_s))
 
-    def logit_grads(quarter, h):
-        cols = slice(h * tok, (h + 1) * tok)
-        block = 2 * quarter + h
-        exp_t = jnp.exp(teacher_ref[block].astype(F32) - scales[quarter, 2:3, cols])
-        grads[block] = (
-            student_exp[block].astype(F32) * scales[quarter, 0:1, cols] - exp_t * scales[quarter, 1:2, cols]
-        ).astype(BF16)
+    def logit_grads(block):
+        scale_s, scale_t, top = [scales[block // 2, block % 2, row : row + 1, :] for row in range(3)]
+        exp_t = jnp.exp(teacher_ref[block].astype(F32) - top)
+        grads[block] = (student_exp[block].astype(F32) * scale_s - exp_t * scale_t).astype(BF16)
 
     def to_neighbour(block, side):
         return ring.copy(
@@ -353,9 +351,8 @@
     def owner_copy(block):
         return dp.copy(gh_mid.at[block], gh_in.at[d], gh_s.at[block], gh_r.at[d], block)
 
-    def hidden_terms(quarter, h):
-        logit_grads(quarter, h)
-        block = 2 * quarter + h
+    def hidden_terms(block):
+        logit_grads(block)
         gh_out[block] = (
             lax.dot_general(
                 grads[block], head_ref[...], (((0,), (0,)), ((), ())), preferred_element_type=F32
@@ -376,17 +373,15 @@
         def _():
             owner_copy(block).start()
 
-    for h in range(2):
-        hidden_terms(m, h)
     student.finish()
     gather_wait(mp, scales.at[m], scales, sc_s, sc_r)
-    order = (m, other_core, other_chip, diagonal)
-    for i in range(1, 4):
-        for h in range(2):
-            hidden_terms(order[i], h)
-            hand_over(2 * order[i - 1] + h)
-    for h in range(2):
-        hand_over(2 * diagonal + h)
+    shifts = ((2, 1), (2, 0), (1, 1), (3, 1), (1, 0), (3, 0), (0, 1), (0, 0))
+    order = [2 * lax.rem(y + dy, n_y) + (d + dx) % 2 for dy, dx in shifts]
+    hidden_terms(order[0])
+    for before, block in zip(order[:-1], order[1:]):
+        hidden_terms(block)
+        hand_over(before)
+    hand_over(order[-1])
 
     scatter_wait(dp, gh_mid, gh_in, gh_s, gh_r)
     gh_in[d] = gh_mid[d]
@@ -486,7 +481,7 @@
                 pltpu.VMEM((n_dp, cols, tok), BF16),
                 pltpu.VMEM((cols, depth), BF16),
                 pltpu.VMEM((n_dp, cols, tok), BF16),
-                pltpu.VMEM((4, 8, own), F32),
+                pltpu.VMEM((4, 2, 8, tok), F32),
                 pltpu.VMEM((n_dp, 4, tok // 4, depth), BF16),
                 pltpu.VMEM((4, 2, cols, tok), F32),
                 pltpu.VMEM((4, cols, tok), F32),

time: 143 us -> 141 us (0.986); the launches traced: 142 us -> 139 us
  Pallas kernels: 142 us -> 138 us
    pallas_call x1, Pallas kernels: 139 us -> 135 us  [per_device(): pl.pallas_call(functools.partial(kernel, (n_dp, n_z, n_zl, n_zh)), name='...]
where the time goes in v7:
time: 141 us; the launch traced here: 139 us
  Pallas kernels  138 us (98%)
    pallas_call x1, Pallas kernels, per_device(): pl.pallas_call(functools.partial(kernel, (n_dp, n_z, n_zl, n_zh)), name='...  135 us

profile of v7, /device:TPU:6, one launch (start us, length us, event | category | flops | bytes accessed | tf_op | source)
XLA Modules:
  0.0 138.5 jit_solution(3635656521380042397)
XLA Ops:
  0.6 135.4 %distill.1 = (f32[1,256]{1,0:T(1,128)}, f32[4,32,896]{2,1,0:T(8,128)}, bf16[594,896]{1,0:T(8,128)(2,1)}) custom-call(bf16[4,32,896]{2,1,0:T(8,128)(2,1)} %bitcast.8, bf16[594,896]{1,0:T(8,128)(2,1)} %bitcast.6, bf16[594,256]{1,0:T(8,128)(2,1)} %bitcast.7, s32[4]{0:T(128)} %start_ref.1), custom_call_target="tpu_custom_call" | custom-call | tf_op jit(solution)/shard_map/distill/pallas_call | solution.py:473
  136.1 2.4 %results.1 = (f32[1,256]{1,0:T(1,128)}, f32[4,32,896]{2,1,0:T(8,128)}, bf16[594,896]{1,0:T(8,128)(2,1)}) custom-call(f32[1,256]{1,0:T(1,128)} %get-tuple-element.9.refs_0_, f32[4,32,896]{2,1,0:T(8,128)} %get-tuple-element.10.refs_1_, bf16[594,896]{1,0:T(8,128)(2,1)} %get-tuple-element.11.refs_2_), custom_call_target="tpu_custom_call" | custom-call | tf_op jit(solution)/shard_map/results/pallas_call | solution.py:527

commit v8 on v7

--- a/solution.py
+++ b/solution.py
@@ -208,8 +208,7 @@
         for peer in column.others():
             to_column(block, peer).start()
     pass_on(partner)
-    if n_zh >= 4:
-        tell(0)
+    tell(0)
     for load in load_teacher:
         load.wait()
     teacher.start()
@@ -239,7 +238,7 @@
         return mp.copy(cross_out.at[k], cross_in.at[k], cross_s.at[k], cross_r.at[k], other_chip)
 
     def partial_sums(k):
-        chip = (1 - x) if k < 2 else x
+        chip = jnp.where(k < 2, 1 - x, x)
 
         def one(j, carry):
             core = jnp.where(j == 0, 1 - c, c)
@@ -257,23 +256,32 @@
         cross_out[k] = parts[k, 1] + swap_in[k]
         cross(k).start()
 
+    def student_step(k, carry):
+        @pl.when(k == 0)
+        def _():
+            arrive(0)
+
+        @pl.when(k == 1)
+        def _():
+            arrive(1)
+
+        partial_sums(k)
+
+        @pl.when(k == 0)
+        def _():
+            forward(1)
+
+        @pl.when(k < 2)
+        def _():
+            send_cross(k)
+            hear(k)
+            tell(k + 1)
+
+        return carry
+
     forward(0)
     load_head.wait()
-    arrive(0)
-    partial_sums(0)
-    forward(1)
-    send_cross(0)
-    if n_zh >= 4:
-        hear(0)
-        tell(1)
-    arrive(1)
-    partial_sums(1)
-    send_cross(1)
-    if n_zh >= 4:
-        hear(1)
-        tell(2)
-    partial_sums(2)
-    partial_sums(3)
+    lax.fori_loop(0, 4, student_step, 0)
     for h in range(2):
         teacher.turn(h)
 
@@ -322,8 +330,7 @@
     store_stats(st_zl.at[mine], share(dp, st_dp, sdp_s, sdp_r))
     student.start()
     store_stats(st_zh.at[zh], share(near, st_zl, szl_s, szl_r))
-    if n_zh >= 4:
-        hear(2)
+    hear(2)
     top_s, sum_s, top_t, sum_t, cross_term = share(far, st_zh, szh_s, szh_r, turns)
     position = lax.broadcasted_iota(jnp.int32, (1, 2 * tok), 1)
     mask = jnp.where(position >= start_ref[m], 1.0, 0.0).astype(F32)
@@ -375,13 +382,22 @@
 
     student.finish()
     gather_wait(mp, scales.at[m], scales, sc_s, sc_r)
-    shifts = ((2, 1), (2, 0), (1, 1), (3, 1), (1, 0), (3, 0), (0, 1), (0, 0))
-    order = [2 * lax.rem(y + dy, n_y) + (d + dx) % 2 for dy, dx in shifts]
-    hidden_terms(order[0])
-    for before, block in zip(order[:-1], order[1:]):
-        hidden_terms(block)
-        hand_over(before)
-    hand_over(order[-1])
+    def block_at(i):
+        pair = i // 2
+        rows_away = jnp.where(pair == 3, 0, jnp.where(pair == 2, 3, 2 - pair))
+        return 2 * ((y + rows_away) % n_y) + (d + 1 + i) % 2
+
+    def grad_step(i, carry):
+        hidden_terms(block_at(i))
+
+        @pl.when(i > 0)
+        def _():
+            hand_over(block_at(i - 1))
+
+        return carry
+
+    lax.fori_loop(0, n_dp, grad_step, 0)
+    hand_over(block_at(n_dp - 1))
 
     scatter_wait(dp, gh_mid, gh_in, gh_s, gh_r)
     gh_in[d] = gh_mid[d]

time: 141 us -> 139 us (0.986); the launches traced: 139 us -> 139 us
  no operation moved by 1% of the time
where the time goes in v8:
time: 139 us
  Pallas kernels  138 us (99%)
    pallas_call x1, Pallas kernels, per_device(): pl.pallas_call(functools.partial(kernel, (n_dp, n_z, n_zl, n_zh)), name='...  136 us

profile of v8, /device:TPU:6, one launch (start us, length us, event | category | flops | bytes accessed | tf_op | source)
XLA Modules:
  0.0 138.6 jit_solution(8826651285801410004)
XLA Ops:
  0.6 135.6 %distill.1 = (f32[1,256]{1,0:T(1,128)}, f32[4,32,896]{2,1,0:T(8,128)}, bf16[594,896]{1,0:T(8,128)(2,1)}) custom-call(bf16[4,32,896]{2,1,0:T(8,128)(2,1)} %bitcast.8, bf16[594,896]{1,0:T(8,128)(2,1)} %bitcast.6, bf16[594,256]{1,0:T(8,128)(2,1)} %bitcast.7, s32[4]{0:T(128)} %start_ref.1), custom_call_target="tpu_custom_call" | custom-call | tf_op jit(solution)/shard_map/distill/pallas_call | solution.py:489
  136.2 2.4 %results.1 = (f32[1,256]{1,0:T(1,128)}, f32[4,32,896]{2,1,0:T(8,128)}, bf16[594,896]{1,0:T(8,128)(2,1)}) custom-call(f32[1,256]{1,0:T(1,128)} %get-tuple-element.9.refs_0_, f32[4,32,896]{2,1,0:T(8,128)} %get-tuple-element.10.refs_1_, bf16[594,896]{1,0:T(8,128)(2,1)} %get-tuple-element.11.refs_2_), custom_call_target="tpu_custom_call" | custom-call | tf_op jit(solution)/shard_map/results/pallas_call | solution.py:543

commit v9 on v8

--- a/solution.py
+++ b/solution.py
@@ -416,8 +416,8 @@
         head_acc[...] += jnp.dot(grads[block], tokens, preferred_element_type=F32)
         return carry
 
-    head_acc[...] = jnp.zeros_like(head_acc)
-    lax.fori_loop(0, n_dp, head_step, 0)
+    head_acc[...] = jnp.dot(grads[0], hid[0].reshape(tok, depth), preferred_element_type=F32)
+    lax.fori_loop(1, n_dp, head_step, 0)
     head_out[...] = head_acc[...].astype(BF16)
     store_head = pltpu.make_async_copy(head_out, grad_head_hbm, local_sem.at[3])
     store_head.start()

time: 139 us -> 140 us (level)
  no operation moved by 1% of the time
where the time goes in v9:
time: 140 us; the launch traced here: 139 us
  Pallas kernels  138 us (99%)
    pallas_call x1, Pallas kernels, per_device(): pl.pallas_call(functools.partial(kernel, (n_dp, n_z, n_zl, n_zh)), name='...  136 us

profile of v9, /device:TPU:6, one launch (start us, length us, event | category | flops | bytes accessed | tf_op | source)
XLA Modules:
  0.0 138.6 jit_solution(13979542057907970012)
XLA Ops:
  0.6 135.6 %distill.1 = (f32[1,256]{1,0:T(1,128)}, f32[4,32,896]{2,1,0:T(8,128)}, bf16[594,896]{1,0:T(8,128)(2,1)}) custom-call(bf16[4,32,896]{2,1,0:T(8,128)(2,1)} %bitcast.8, bf16[594,896]{1,0:T(8,128)(2,1)} %bitcast.6, bf16[594,256]{1,0:T(8,128)(2,1)} %bitcast.7, s32[4]{0:T(128)} %start_ref.1), custom_call_target="tpu_custom_call" | custom-call | tf_op jit(solution)/shard_map/distill/pallas_call | solution.py:489
  136.2 2.4 %results.1 = (f32[1,256]{1,0:T(1,128)}, f32[4,32,896]{2,1,0:T(8,128)}, bf16[594,896]{1,0:T(8,128)(2,1)}) custom-call(f32[1,256]{1,0:T(1,128)} %get-tuple-element.9.refs_0_, f32[4,32,896]{2,1,0:T(8,128)} %get-tuple-element.10.refs_1_, bf16[594,896]{1,0:T(8,128)(2,1)} %get-tuple-element.11.refs_2_), custom_call_target="tpu_custom_call" | custom-call | tf_op jit(solution)/shard_map/results/pallas_call | solution.py:543
